TPU v7x, 512 devices: a whole 4x8x8 slice. The times are simulated.
512 devices in a mesh: fsdp: 32 (over z_lo, x, core), seq: 16 (over y, z_hi).
Axes of the slice: x: 4, y: 8, z: 8 (z_hi: 2, z_lo: 4; z = z_hi * 4 + z_lo), core: 2. Of those that a mesh axis runs over, the one named last changes fastest.
Arguments:
- streams: bfloat16 [3, 8192, 4096], P(None, 'seq', 'fsdp'), may hold values from -6 to 6
- record_blocks: int32 [3], replicated, may hold values from 1 to 32, as said below
- tail_rows: int32 [3], replicated, may hold values from 1 to 128
- unit_dest: int32 [512], replicated, may hold values from 0 to 511, as said below
- mixer_filter: float32 [128, 4096], P(None, ('fsdp', 'seq')), may hold values from -0.5 to 0.5
- feat_filter: float32 [7, 3, 4096], P(None, None, ('fsdp', 'seq')), may hold values from -2 to 2
- norm_gain: float32 [4096], P(('fsdp', 'seq')), may hold values from 0.25 to 1.75
- out_grad: bfloat16 [8192, 4096], P('seq', 'fsdp'), may hold values from -6 to 6
Outputs:
- out: bfloat16 [8192, 4096], P('seq', 'fsdp')
- stream_grad: bfloat16 [3, 8192, 4096], P(None, 'seq', 'fsdp')
- mixer_grad: float32 [128, 4096], P(None, ('fsdp', 'seq'))
- feat_grad: float32 [7, 3, 4096], P(None, None, ('fsdp', 'seq'))
- gain_grad: float32 [4096], P(('fsdp', 'seq'))
Inputs may be any that keep to these rules, and one draw needn't show every extreme that they name: unit_dest is a permutation; the 32 units of each shard of 512 rows go to exactly half of the shards, 4 units to each of them, so each shard receives 4 units from each of half of the shards. record_blocks sums to 64; the second record is the longest, exactly 32 blocks.
All inputs are finite; a program needn't handle non-finite values.
Results may differ from a plain program's by a relative error of at most 0.0085.
Values may be sent and summed in bfloat16 or wider, within the bound.
A program may use at most 64 MiB of HBM per device.

v0:
```python
import jax
import jax.numpy as jnp
import numpy as np
from jax import lax
from jax.sharding import PartitionSpec as P

C = 4096
KM = 128
KF = 7
UNIT = 16


EPSILON = 1e-06


def from_behind(array, axis, by):
    length = lax.axis_size(axis)
    pairs = [(i, i + by) for i in range(length) if 0 <= i + by < length]
    return lax.ppermute(array, axis, pairs)


def lag_table(length):
    row_index = np.arange(length)[:, None]
    col_index = np.arange(2 * length)[None, :]
    lagged = length + row_index - col_index
    return np.where((lagged >= 0) & (lagged < length), lagged, length).astype(np.int32)


def toeplitz(filter_bf):
    padded = jnp.concatenate(
        [filter_bf.T, jnp.zeros((filter_bf.shape[1], 1), filter_bf.dtype)], axis=1
    )
    return jnp.take(padded, jnp.asarray(lag_table(filter_bf.shape[0])), axis=1)


def record_masks(record_blocks, tail_rows, first_block, block_count):
    starts = jnp.cumsum(record_blocks) - record_blocks
    record_ends = starts + record_blocks - 1
    block_ids = first_block + jnp.arange(block_count, dtype=jnp.int32)
    starts_here = jnp.any(starts[None, :] == block_ids[:, None], axis=1)
    starts_next = jnp.any(starts[None, :] == block_ids[:, None] + 1, axis=1)
    closing = record_ends[None, :] == block_ids[:, None]
    filled_rows = jnp.where(
        jnp.any(closing, axis=1), jnp.sum(jnp.where(closing, tail_rows[None, :], 0), axis=1), KM
    )
    live_rows = (jnp.arange(KM, dtype=jnp.int32)[None, :] < filled_rows[:, None]).astype(
        jnp.float32
    )
    carry_on = 1.0 - starts_here.astype(jnp.float32)
    carry_next = 1.0 - starts_next.astype(jnp.float32)
    return (carry_on, carry_next, live_rows)


def routing(unit_dest, position, shards, per_shard, capacity):
    target_shard = (unit_dest // per_shard).reshape(shards, per_shard)
    unit_ids = jnp.arange(per_shard, dtype=jnp.int32)
    earlier = unit_ids[None, :] < unit_ids[:, None]
    same_target = target_shard[:, :, None] == target_shard[:, None, :]
    rank_within = jnp.sum(jnp.where(same_target & earlier[None], 1, 0), axis=2).astype(jnp.int32)
    own_target = lax.dynamic_index_in_dim(target_shard, position, 0, keepdims=False)
    own_rank = lax.dynamic_index_in_dim(rank_within, position, 0, keepdims=False)
    own_slot = own_target * capacity + own_rank
    slot_ids = jnp.arange(shards * capacity, dtype=jnp.int32)
    send_match = own_slot[None, :] == slot_ids[:, None]
    send_source = jnp.sum(jnp.where(send_match, unit_ids[None, :], 0), axis=1)
    send_filled = jnp.any(send_match, axis=1)
    arrive_slot = (jnp.arange(shards, dtype=jnp.int32)[:, None] * capacity + rank_within).reshape(
        -1
    )
    wanted = position * per_shard + unit_ids
    arrive_match = unit_dest[None, :] == wanted[:, None]
    packed_slot = jnp.sum(jnp.where(arrive_match, arrive_slot[None, :], 0), axis=1)
    back_match = packed_slot[None, :] == slot_ids[:, None]
    back_source = jnp.sum(jnp.where(back_match, unit_ids[None, :], 0), axis=1)
    back_filled = jnp.any(back_match, axis=1)
    return (send_source, send_filled, packed_slot, back_source, back_filled, own_slot)


def move_units(values, source, filled, shards):
    unit_rows = values.reshape(values.shape[0], -1, UNIT, values.shape[2])
    picked = jnp.take(unit_rows, source, axis=1)
    picked = jnp.where(filled[None, :, None, None], picked, jnp.zeros_like(picked))
    return picked.reshape(values.shape[0], shards, -1, values.shape[2])


def featurize(extended, feat_taps, live_rows):
    accumulated = jnp.zeros(extended.shape[:2] + (KM, extended.shape[3]), jnp.float32)
    for tap_index in range(KF):
        window = extended[:, :, 8 - tap_index : 8 - tap_index + KM].astype(jnp.float32)
        accumulated = accumulated + feat_taps[tap_index][:, None, None, :] * window
    return (accumulated * live_rows[None, :, :, None]).astype(jnp.bfloat16)


def spread(d_extended, feat_taps):
    accumulated = jnp.zeros(d_extended.shape[:2] + (KM, d_extended.shape[3]), jnp.float32)
    for tap_index in range(KF):
        window = d_extended[:, :, tap_index : tap_index + KM].astype(jnp.float32)
        accumulated = accumulated + feat_taps[tap_index][:, None, None, :] * window
    return accumulated.astype(jnp.bfloat16)


def tap_sums(d_feature, extended):
    d_float = d_feature.astype(jnp.float32)
    collected = []
    for tap_index in range(KF):
        window = extended[:, :, 8 - tap_index : 8 - tap_index + KM].astype(jnp.float32)
        collected.append(jnp.sum(d_float * window, axis=(1, 2)))
    return jnp.stack(collected)


def lag_sums(d_response, both_parts):
    channels = d_response.shape[2]
    group_width = min(32, channels)
    collected = []
    for start_col in range(0, channels, group_width):
        products = jnp.einsum(
            "bic,bkc->cik",
            d_response[:, :, start_col : start_col + group_width],
            both_parts[:, :, start_col : start_col + group_width],
            preferred_element_type=jnp.float32,
        )
        flattened = jnp.pad(products.reshape(group_width, 2 * KM * KM), ((0, 0), (0, KM)))
        skewed = flattened.reshape(group_width, KM, 2 * KM + 1)
        summed = jnp.sum(skewed[:, :, 1 : KM + 1], axis=1)
        collected.append(summed[:, ::-1].T)
    return jnp.concatenate(collected, axis=1)


def body(
    streams, record_blocks, tail_rows, unit_dest, mixer_filter, feat_filter, norm_gain, out_grad
):
    rows_dev = streams.shape[1]
    channels = streams.shape[2]
    shards = lax.axis_size("seq")
    position = lax.axis_index("seq")
    per_shard = rows_dev // UNIT
    capacity = 2 * per_shard // shards
    blocks_dev = rows_dev // KM
    send_source, send_filled, packed_slot, back_source, back_filled, own_slot = routing(
        unit_dest, position, shards, per_shard, capacity
    )
    outgoing = move_units(streams, send_source, send_filled, shards)
    arrived = lax.all_to_all(outgoing, "seq", split_axis=1, concat_axis=1, tiled=True)
    packed = jnp.take(arrived.reshape(3, -1, UNIT, channels), packed_slot, axis=1).reshape(
        3, blocks_dev, KM, channels
    )
    carry_on, carry_next, live_rows = record_masks(
        record_blocks, tail_rows, position * blocks_dev, blocks_dev
    )
    mixer_panel, feat_panel, gain_panel = (
        lax.all_gather(mixer_filter, "seq", axis=1, tiled=True),
        lax.all_gather(feat_filter, "seq", axis=2, tiled=True),
        lax.all_gather(norm_gain, "seq", axis=0, tiled=True),
    )
    rim_rows = from_behind(packed[:, blocks_dev - 1, KM - 8 :, :], "seq", 1)
    tail_part = jnp.concatenate([rim_rows[:, None], packed[:, : blocks_dev - 1, KM - 8 :]], axis=1)
    tail_part = jnp.where(carry_on[None, :, None, None] > 0, tail_part, jnp.zeros_like(tail_part))
    extended = jnp.concatenate([tail_part, packed], axis=2)
    feature = featurize(extended, feat_panel, live_rows)
    mixed_in = (feature[1].astype(jnp.float32) * feature[2].astype(jnp.float32)).astype(
        jnp.bfloat16
    )
    matrix = toeplitz(mixer_panel.astype(jnp.bfloat16))
    rim_mixed = from_behind(mixed_in[blocks_dev - 1], "seq", 1)
    previous = jnp.concatenate([rim_mixed[None], mixed_in[: blocks_dev - 1]], axis=0)
    previous = jnp.where(carry_on[:, None, None] > 0, previous, jnp.zeros_like(previous))
    response = jnp.einsum(
        "cik,bkc->bic", matrix[:, :, KM:], mixed_in, preferred_element_type=jnp.float32
    )
    response = response + jnp.einsum(
        "cik,bkc->bic", matrix[:, :, :KM], previous, preferred_element_type=jnp.float32
    )
    gated_out = (feature[0].astype(jnp.float32) * response).astype(jnp.bfloat16)
    gated_float = gated_out.astype(jnp.float32)
    squares = lax.psum(jnp.sum(gated_float * gated_float, axis=-1), "fsdp")
    row_scale = live_rows * lax.rsqrt(squares / C + EPSILON)
    normed = gated_float * row_scale[..., None]
    out = (normed * gain_panel).astype(jnp.bfloat16).reshape(rows_dev, channels)
    mixer_back, feat_back, gain_back = (
        lax.all_gather(mixer_filter, "seq", axis=1, tiled=True),
        lax.all_gather(feat_filter, "seq", axis=2, tiled=True),
        lax.all_gather(norm_gain, "seq", axis=0, tiled=True),
    )
    matrix_back = toeplitz(mixer_back.astype(jnp.bfloat16))
    grad_rows = out_grad.reshape(blocks_dev, KM, channels).astype(jnp.float32)
    gain_term = jnp.sum(grad_rows * normed, axis=(0, 1))
    weighted = grad_rows * gain_back
    inner_sum = lax.psum(jnp.sum(weighted * normed, axis=-1), "fsdp") / C
    d_gated = (row_scale[..., None] * (weighted - normed * inner_sum[..., None])).astype(
        jnp.bfloat16
    )
    d_gated_float = d_gated.astype(jnp.float32)
    d_query = d_gated_float * response
    d_response = (d_gated_float * feature[0].astype(jnp.float32)).astype(jnp.bfloat16)
    response_rim = from_behind(d_response[0], "seq", -1)
    following = jnp.concatenate([d_response[1:], response_rim[None]], axis=0)
    following = jnp.where(carry_next[:, None, None] > 0, following, jnp.zeros_like(following))
    d_mixed = jnp.einsum(
        "cik,bic->bkc", matrix_back[:, :, KM:], d_response, preferred_element_type=jnp.float32
    )
    d_mixed = d_mixed + jnp.einsum(
        "cik,bic->bkc", matrix_back[:, :, :KM], following, preferred_element_type=jnp.float32
    )
    d_feature = jnp.stack(
        [
            d_query,
            d_mixed * feature[2].astype(jnp.float32),
            d_mixed * feature[1].astype(jnp.float32),
        ]
    ).astype(jnp.bfloat16)
    mixer_term = lag_sums(d_response, jnp.concatenate([previous, mixed_in], axis=1))
    feat_term = tap_sums(d_feature, extended)
    feature_rim = from_behind(d_feature[:, 0, :8, :], "seq", -1)
    head_rows = jnp.concatenate([d_feature[:, 1:, :8], feature_rim[:, None]], axis=1)
    head_rows = jnp.where(carry_next[None, :, None, None] > 0, head_rows, jnp.zeros_like(head_rows))
    d_extended = jnp.concatenate([d_feature, head_rows], axis=2)
    d_packed = spread(d_extended, feat_back).reshape(3, rows_dev, channels)
    returning = move_units(d_packed, back_source, back_filled, shards)
    returned = lax.all_to_all(returning, "seq", split_axis=1, concat_axis=1, tiled=True)
    stream_grad = jnp.take(returned.reshape(3, -1, UNIT, channels), own_slot, axis=1).reshape(
        3, rows_dev, channels
    )
    mixer_whole, feat_whole, gain_whole = lax.psum((mixer_term, feat_term, gain_term), "seq")
    piece_width = channels // shards
    first_col = position * piece_width
    mixer_grad = lax.dynamic_slice_in_dim(mixer_whole, first_col, piece_width, 1)
    feat_grad = lax.dynamic_slice_in_dim(feat_whole, first_col, piece_width, 2)
    gain_grad = lax.dynamic_slice_in_dim(gain_whole, first_col, piece_width, 0)
    return (out, stream_grad, mixer_grad, feat_grad, gain_grad)


def solution(mesh):
    placed = (
        P(None, "seq", "fsdp"),
        P(),
        P(),
        P(),
        P(None, ("fsdp", "seq")),
        P(None, None, ("fsdp", "seq")),
        P(("fsdp", "seq")),
        P("seq", "fsdp"),
    )
    return jax.shard_map(
        body,
        mesh=mesh,
        in_specs=placed,
        out_specs=(
            P("seq", "fsdp"),
            P(None, "seq", "fsdp"),
            P(None, ("fsdp", "seq")),
            P(None, None, ("fsdp", "seq")),
            P(("fsdp", "seq")),
        ),
        check_vma=False,
    )
```

profile of v0, /device:TPU:2, one launch (start us, length us, event | category | flops | bytes accessed | tf_op | source)
XLA Modules:
  0.0 794.0 jit_solution(134356089748451770)
XLA Ops:
  13.5 15.6 %all-to-all-start = ((bf16[3,16,64,128]{3,2,0,1:T(8,128)(2,1)}), bf16[3,16,64,128]{3,2,0,1:T(8,128)(2,1)S(1)}, u32[]{:S(2)}, u32[]{:S(2)}) async-start(bf16[3,16,64,128]{3,2,0,1:T(8,128)(2,1)} %copy.175), calls=%async_computation | async-start | bytes 1572864 | tf_op jit(solution)/shard_map/all_to_all | solution.py:143
  31.7 67.7 %all_gather.12 = f32[7,3,128]{0,1,2:T(4,128)S(1)} all-gather(f32[7,3,8]{0,1,2:T(4,128)S(1)} %copy.172), channel_id=1, replica_groups=mesh['fsdp'=32,'seq'=16] {'seq'}, dimensions={2}, use_global_device_ids=true | all-gather | bytes 11424 | tf_op jit(solution)/shard_map/all_gather | solution.py:152
  103.8 5.5 collective-permute-start
  113.4 6.0 fusion.40
  119.6 5.7 collective-permute-start.1
  126.6 47.5 %all_gather.13 = bf16[128,128]{0,1:T(8,128)(2,1)S(1)} all-gather(bf16[128,8]{0,1:T(8,128)(2,1)S(1)} %convert.55), channel_id=1, replica_groups=mesh['fsdp'=32,'seq'=16] {'seq'}, dimensions={1}, use_global_device_ids=true | all-gather | bytes 34816 | tf_op jit(solution)/shard_map/all_gather | solution.py:151
  174.2 114.1 %gather_fusion.2 = bf16[32768,128]{1,0:T(8,128)(2,1)} fusion(bf16[128,129]{0,1:T(8,128)(2,1)S(1)} %concatenate.32, s32[32768]{0:T(1024)S(1)} %copy-done.8), kind=kCustom, calls=%fused_computation.2.clone | custom fusion | bytes 16908288 | tf_op jit(solution)/shard_map/jit(_take)/gather | solution.py:33
  288.4 12.4 %copy.213 = bf16[128,256,128]{1,0,2:T(8,128)(2,1)} copy(bf16[128,256,128]{2,1,0:T(8,128)(2,1)} %bitcast.135) | data formatting | bytes 16777216 | tf_op jit(solution)/shard_map/jit(_take)/gather | solution.py:33
  303.1 49.9 %all-reduce.5 = f32[128]{0:T(128)S(1)} all-reduce(f32[128]{0:T(128)S(1)} %dynamic-update-slice), channel_id=1, replica_groups=mesh['fsdp'=32,'seq'=16] {'seq'}, use_global_device_ids=true, to_apply=%add.5 | all-reduce | flops 128 | bytes 1024
  353.5 4.4 fusion.2
  358.0 4.5 fusion.56
  362.5 61.7 %psum.35 = f32[4,128]{1,0:T(4,128)S(1)} all-reduce(f32[4,128]{1,0:T(4,128)S(1)} %get-tuple-element.51), channel_id=1, replica_groups=mesh['fsdp'=32,'seq'=16] {'fsdp'}, use_global_device_ids=true, to_apply=%region_9.13 | all-reduce | flops 512 | bytes 4096 | tf_op jit(solution)/shard_map/psum | solution.py:175
  425.3 67.4 %psum.36 = f32[4,128]{1,0:T(4,128)S(1)} all-reduce(f32[4,128]{1,0:T(4,128)S(1)} %get-tuple-element.40), channel_id=1, replica_groups=mesh['fsdp'=32,'seq'=16] {'fsdp'}, use_global_device_ids=true, to_apply=%region_12.16 | all-reduce | flops 512 | bytes 4096 | tf_op jit(solution)/shard_map/psum | solution.py:188
  493.2 12.0 %collective-permute-start.2 = (bf16[128,128]{1,0:T(8,128)(2,1)S(1)}, bf16[128,128]{1,0:T(8,128)(2,1)S(1)}, u32[]{:S(2)}, u32[]{:S(2)}) collective-permute-start(bf16[128,128]{1,0:T(8,128)(2,1)S(1)} %bitcast.174), channel_id=1, source_target_pairs={{1,0},{2,1},{3,2},{4,3},{5,4},{6,5},{7,6},{8,7},{9,8},{10,9},{11,1... | collective-permute-start | bytes 98312 | tf_op jit(solution)/shard_map/ppermute | solution.py:19
  506.0 2.4 copy.214
  510.7 8.0 %reshape.241 = f32[32,128,257]{2,1,0:T(8,128)} reshape(f32[32,32896]{1,0:T(8,128)} %pad.14) | data formatting | bytes 8421376 | tf_op jit(solution)/shard_map/reshape | solution.py:123
  518.6 2.8 slice_reduce_fusion.3
  522.3 2.4 copy.215
  527.0 8.0 %reshape.243 = f32[32,128,257]{2,1,0:T(8,128)} reshape(f32[32,32896]{1,0:T(8,128)} %pad.15) | data formatting | bytes 8421376 | tf_op jit(solution)/shard_map/reshape | solution.py:123
  534.9 2.8 slice_reduce_fusion.2
  543.3 8.0 %reshape.245 = f32[32,128,257]{2,1,0:T(8,128)} reshape(f32[32,32896]{1,0:T(8,128)} %pad.16) | data formatting | bytes 8421376 | tf_op jit(solution)/shard_map/reshape | solution.py:123
  551.2 2.8 slice_reduce_fusion.1
  559.6 8.0 %reshape.247 = f32[32,128,257]{2,1,0:T(8,128)} reshape(f32[32,32896]{1,0:T(8,128)} %pad.17) | data formatting | bytes 8421376 | tf_op jit(solution)/shard_map/reshape | solution.py:123
  567.6 2.8 slice_reduce_fusion
  572.3 3.5 fusion
  575.7 3.5 fusion.60
  579.6 7.8 fusion.38
  589.9 7.9 collective-permute-done.3
  598.6 4.7 fusion.39
  605.8 13.2 %all-to-all-start.1 = ((bf16[3,16,64,128]{3,2,0,1:T(8,128)(2,1)}), bf16[3,16,64,128]{3,2,0,1:T(8,128)(2,1)S(1)}, u32[]{:S(2)}, u32[]{:S(2)}) async-start(bf16[3,16,64,128]{3,2,0,1:T(8,128)(2,1)} %copy.202), calls=%async_computation.1 | async-start | bytes 1572864 | tf_op jit(solution)/shard_map/all_to_all | solution.py:219
  619.1 104.2 %all-reduce.6 = (f32[7,3,128]{2,1,0:T(4,128)S(1)}, f32[128]{0:T(128)S(1)}) all-reduce(f32[7,3,128]{2,1,0:T(4,128)S(1)} %constant_dynamic-update-slice_fusion, f32[128]{0:T(128)S(1)} %get-tuple-element.39), channel_id=1, replica_groups=mesh['fsdp'=32,'seq'=16] {'seq'}, use_global_device_ids=true, to_apply=%region_27.31 | all-reduce | flops 2816 | bytes 22528 | tf_op jit(solution)/shard_map/psum | solution.py:223
  724.6 59.1 %all-reduce.9.cloned.1.call-done = f32[128,128]{0,1:T(8,128)} async-done(((f32[128,128]{0,1:T(8,128)}), f32[128,128]{0,1:T(8,128)}) %all-reduce.9.cloned.1.call-update) | async-done | bytes 65552 | tf_op jit(solution)/shard_map/psum | solution.py:223
  (209 shorter events, 51.7 us)
Async XLA Ops:
  7.2 23.8 %copy-start.34 = (s32[3]{0:T(128)S(1)}, s32[3]{0:T(128)}, u32[]{:S(2)}) copy-start(s32[3]{0:T(128)} %param.17) | copy-start | bytes 40
  7.2 24.2 %copy-start.35 = (s32[3]{0:T(128)S(1)}, s32[3]{0:T(128)}, u32[]{:S(2)}) copy-start(s32[3]{0:T(128)} %param.18) | copy-start | bytes 40
  7.2 24.4 %copy-start.25 = (f32[7,3,8]{2,0,1:T(8,128)S(1)}, f32[7,3,8]{2,0,1:T(8,128)}, u32[]{:S(2)}) copy-start(f32[7,3,8]{2,0,1:T(8,128)} %param.21) | copy-start | bytes 2020
  12.4 89.2 %copy-start.10 = (s32[32768]{0:T(1024)S(1)}, s32[32768]{0:T(1024)}, u32[]{:S(2)}) copy-start(s32[32768]{0:T(1024)} %constant.126) | copy-start | bytes 393220
  13.5 88.8 %all-to-all-start = ((bf16[3,16,64,128]{3,2,0,1:T(8,128)(2,1)}), bf16[3,16,64,128]{3,2,0,1:T(8,128)(2,1)S(1)}, u32[]{:S(2)}, u32[]{:S(2)}) async-start(bf16[3,16,64,128]{3,2,0,1:T(8,128)(2,1)} %copy.175), calls=%async_computation | async-start | bytes 1572864 | tf_op jit(solution)/shard_map/all_to_all | solution.py:143
  29.1 754.5 %all-reduce.9.cloned.1.call-start = ((), (), s32[]{:S(2)}) async-start(), calls=%async_computation.2 | async-start | bytes 131072 | tf_op jit(solution)/shard_map/psum | solution.py:223
  102.3 24.3 %copy-start.26 = (f32[128,8]{0,1:T(8,128)S(1)}, f32[128,8]{0,1:T(8,128)}, u32[]{:S(2)}) copy-start(f32[128,8]{0,1:T(8,128)} %param.20) | copy-start | bytes 12292
  102.3 71.9 %copy-start.8 = (s32[32768]{0:T(1024)S(1)}, s32[32768]{0:T(1024)}, u32[]{:S(2)}) copy-start(s32[32768]{0:T(1024)} %broadcast_clamp_fusion) | copy-start | bytes 393220
  103.8 8.9 %collective-permute-start = (bf16[3,8,128]{2,1,0:T(8,128)(2,1)S(1)}, bf16[3,8,128]{2,1,0:T(8,128)(2,1)S(1)}, u32[]{:S(2)}, u32[]{:S(2)}) collective-permute-start(bf16[3,8,128]{2,1,0:T(8,128)(2,1)S(1)} %slice_bitcast_fusion.3), channel_id=1, source_target_pairs={{0,1},{1,2},{2,3},{3,4},{4,5},{5,6},{6,7},{7,8},{8,9},{9,10},{10,1... | collective-permute-start | bytes 18440 | tf_op jit(solution)/shard_map/ppermute | solution.py:19
  111.5 176.8 %copy-start.11 = (f32[1,3,128]{2,1,0:T(4,128)}, f32[1,3,128]{2,1,0:T(4,128)S(1)}, u32[]{:S(2)}) copy-start(f32[1,3,128]{2,1,0:T(4,128)S(1)} %copy.173) | copy-start | bytes 4612
  111.7 176.7 %copy-start.13 = (f32[1,3,128]{2,1,0:T(4,128)}, f32[1,3,128]{2,1,0:T(4,128)S(1)}, u32[]{:S(2)}) copy-start(f32[1,3,128]{2,1,0:T(4,128)S(1)} %copy.183) | copy-start | bytes 4612
  111.8 176.5 %copy-start.15 = (f32[1,3,128]{2,1,0:T(4,128)}, f32[1,3,128]{2,1,0:T(4,128)S(1)}, u32[]{:S(2)}) copy-start(f32[1,3,128]{2,1,0:T(4,128)S(1)} %copy.184) | copy-start | bytes 4612
  111.9 176.4 %copy-start.17 = (f32[1,3,128]{2,1,0:T(4,128)}, f32[1,3,128]{2,1,0:T(4,128)S(1)}, u32[]{:S(2)}) copy-start(f32[1,3,128]{2,1,0:T(4,128)S(1)} %copy.185) | copy-start | bytes 4612
  112.1 176.3 %copy-start.19 = (f32[1,3,128]{2,1,0:T(4,128)}, f32[1,3,128]{2,1,0:T(4,128)S(1)}, u32[]{:S(2)}) copy-start(f32[1,3,128]{2,1,0:T(4,128)S(1)} %copy.186) | copy-start | bytes 4612
  112.2 176.2 %copy-start.21 = (f32[1,3,128]{2,1,0:T(4,128)}, f32[1,3,128]{2,1,0:T(4,128)S(1)}, u32[]{:S(2)}) copy-start(f32[1,3,128]{2,1,0:T(4,128)S(1)} %copy.187) | copy-start | bytes 4612
  112.3 176.0 %copy-start.23 = (f32[1,3,128]{2,1,0:T(4,128)}, f32[1,3,128]{2,1,0:T(4,128)S(1)}, u32[]{:S(2)}) copy-start(f32[1,3,128]{2,1,0:T(4,128)S(1)} %copy.179) | copy-start | bytes 4612
  113.0 175.4 %copy-start.4 = (bf16[3,4,8,128]{2,1,3,0:T(4,128)(2,1)}, bf16[3,4,8,128]{2,1,3,0:T(4,128)(2,1)S(1)}, u32[]{:S(2)}) copy-start(bf16[3,4,8,128]{2,1,3,0:T(4,128)(2,1)S(1)} %copy.181) | copy-start | bytes 73732
  119.6 233.4 %collective-permute-start.1 = (bf16[128,128]{1,0:T(8,128)(2,1)S(1)}, bf16[128,128]{1,0:T(8,128)(2,1)S(1)}, u32[]{:S(2)}, u32[]{:S(2)}) collective-permute-start(bf16[128,128]{1,0:T(8,128)(2,1)S(1)} %bitcast.176), channel_id=1, source_target_pairs={{0,1},{1,2},{2,3},{3,4},{4,5},{5,6},{6,7},{7,8},{8,9},{9,10},{10,1... | collective-permute-start | bytes 98312 | tf_op jit(solution)/shard_map/ppermute | solution.py:19
  353.5 70.7 %copy-start.29 = (s32[4]{0:T(128)S(1)}, s32[4]{0:T(128)}, u32[]{:S(2)}) copy-start(s32[4]{0:T(128)} %copy-done.28) | copy-start | bytes 52
  493.2 78.9 %collective-permute-start.2 = (bf16[128,128]{1,0:T(8,128)(2,1)S(1)}, bf16[128,128]{1,0:T(8,128)(2,1)S(1)}, u32[]{:S(2)}, u32[]{:S(2)}) collective-permute-start(bf16[128,128]{1,0:T(8,128)(2,1)S(1)} %bitcast.174), channel_id=1, source_target_pairs={{1,0},{2,1},{3,2},{4,3},{5,4},{6,5},{7,6},{8,7},{9,8},{10,9},{11,1... | collective-permute-start | bytes 98312 | tf_op jit(solution)/shard_map/ppermute | solution.py:19
  579.2 19.4 %copy-start.12 = (f32[1,3,128]{2,1,0:T(4,128)S(1)}, f32[1,3,128]{2,1,0:T(4,128)}, u32[]{:S(2)}) copy-start(f32[1,3,128]{2,1,0:T(4,128)} %copy-done.11) | copy-start | bytes 4612
  579.2 19.4 %copy-start.14 = (f32[1,3,128]{2,1,0:T(4,128)S(1)}, f32[1,3,128]{2,1,0:T(4,128)}, u32[]{:S(2)}) copy-start(f32[1,3,128]{2,1,0:T(4,128)} %copy-done.13) | copy-start | bytes 4612
  579.2 19.4 %copy-start.16 = (f32[1,3,128]{2,1,0:T(4,128)S(1)}, f32[1,3,128]{2,1,0:T(4,128)}, u32[]{:S(2)}) copy-start(f32[1,3,128]{2,1,0:T(4,128)} %copy-done.15) | copy-start | bytes 4612
  579.2 19.4 %copy-start.18 = (f32[1,3,128]{2,1,0:T(4,128)S(1)}, f32[1,3,128]{2,1,0:T(4,128)}, u32[]{:S(2)}) copy-start(f32[1,3,128]{2,1,0:T(4,128)} %copy-done.17) | copy-start | bytes 4612
  579.2 19.4 %copy-start.20 = (f32[1,3,128]{2,1,0:T(4,128)S(1)}, f32[1,3,128]{2,1,0:T(4,128)}, u32[]{:S(2)}) copy-start(f32[1,3,128]{2,1,0:T(4,128)} %copy-done.19) | copy-start | bytes 4612
  579.2 19.4 %copy-start.22 = (f32[1,3,128]{2,1,0:T(4,128)S(1)}, f32[1,3,128]{2,1,0:T(4,128)}, u32[]{:S(2)}) copy-start(f32[1,3,128]{2,1,0:T(4,128)} %copy-done.21) | copy-start | bytes 4612
  579.2 19.4 %copy-start.24 = (f32[1,3,128]{2,1,0:T(4,128)S(1)}, f32[1,3,128]{2,1,0:T(4,128)}, u32[]{:S(2)}) copy-start(f32[1,3,128]{2,1,0:T(4,128)} %copy-done.23) | copy-start | bytes 4612
  587.6 10.2 %collective-permute-start.3 = (bf16[3,8,128]{2,1,0:T(8,128)(2,1)S(1)}, bf16[3,8,128]{2,1,0:T(8,128)(2,1)S(1)}, u32[]{:S(2)}, u32[]{:S(2)}) collective-permute-start(bf16[3,8,128]{2,1,0:T(8,128)(2,1)S(1)} %bitcast.192), channel_id=1, source_target_pairs={{1,0},{2,1},{3,2},{4,3},{5,4},{6,5},{7,6},{8,7},{9,8},{10,9},{11,1... | collective-permute-start | bytes 18440 | tf_op jit(solution)/shard_map/ppermute | solution.py:19
  589.4 15.1 %copy-start.32 = (pred[64]{0:T(512)(128)(4,1)S(1)}, pred[64]{0:T(512)(128)(4,1)}, u32[]{:S(2)}) copy-start(pred[64]{0:T(512)(128)(4,1)} %fusion.78) | copy-start | bytes 196
  604.5 181.3 %copy-start.30 = (pred[32]{0:T(512)(128)(4,1)S(1)}, pred[32]{0:T(512)(128)(4,1)}, u32[]{:S(2)}) copy-start(pred[32]{0:T(512)(128)(4,1)} %get-tuple-element.47) | copy-start | bytes 100
  604.5 182.1 %copy-start.1 = (bf16[3,512,128]{2,1,0:T(8,128)(2,1)S(1)}, bf16[3,512,128]{2,1,0:T(8,128)(2,1)}, u32[]{:S(2)}) copy-start(bf16[3,512,128]{2,1,0:T(8,128)(2,1)} %param.16) | copy-start | bytes 1179652
  605.8 179.1 %all-to-all-start.1 = ((bf16[3,16,64,128]{3,2,0,1:T(8,128)(2,1)}), bf16[3,16,64,128]{3,2,0,1:T(8,128)(2,1)S(1)}, u32[]{:S(2)}, u32[]{:S(2)}) async-start(bf16[3,16,64,128]{3,2,0,1:T(8,128)(2,1)} %copy.202), calls=%async_computation.1 | async-start | bytes 1572864 | tf_op jit(solution)/shard_map/all_to_all | solution.py:219
  (12 other events, 112.0 us)
Sparse Core Ops, SparseCore 0:
  571.4 212.1 all-reduce.8
where the time goes:
time: 797 us; the launch traced here: 794 us
  blocking collectives  399 us (50%)
  local copies, waits for them, and re-layouts  195 us (24%)
  waiting for transfers between devices  67 us (8%)
  starting transfers between devices  53.5 us (7%)
  other arithmetic  44.4 us (6%)
  matrix products  19 us (2%)
  between operations  16.1 us (2%)
    gather x2, local copies, waits for them, and re-layouts, toeplitz(): return jnp.take(padded, jnp.asarray(lag_table(filter_bf.shape[0])), axis=1)  126 us
    psum x1, blocking collectives, body(): lax.psum((mixer_term, feat_term, gain_term), 'seq')  104 us
    all_gather x1, blocking collectives, body(): lax.all_gather(feat_filter, 'seq', axis=2, tiled=True)  67.7 us
    psum x1, blocking collectives, body(): inner_sum = lax.psum(jnp.sum(weighted * normed, axis=-1), 'fsdp') / C  67.4 us
    psum x1, blocking collectives, body(): squares = lax.psum(jnp.sum(gated_float * gated_float, axis=-1), 'fsdp')  61.7 us
    psum x1, waiting for transfers between devices, body(): lax.psum((mixer_term, feat_term, gain_term), 'seq')  59.1 us
    unnamed x1, blocking collectives  49.9 us
    all_gather x1, blocking collectives, body(): lax.all_gather(mixer_filter, 'seq', axis=1, tiled=True)  47.5 us
  transfers between devices with their start and end apart: 7, of which 2 were waited for; matrix products, arithmetic and copies ran while one was open for 29% of the time, Pallas kernels for 0%

commit v1 on v0

v1 whole, which is shorter than its diff:
```python
import functools

import jax
import jax.numpy as jnp
from jax import lax
from jax.experimental import pallas as pl
from jax.experimental.pallas import tpu as pltpu
from jax.sharding import PartitionSpec as P

C = 4096
KM = 128
KF = 7
UNIT = 16
CAP = 4
EPSILON = 1e-06
INTERPRET = False

F32 = jnp.float32
BF16 = jnp.bfloat16
VMEM = pl.BlockSpec(memory_space=pltpu.VMEM)
SMEM = pl.BlockSpec(memory_space=pltpu.SMEM)

LANES = 128
BLOCKS = 4
ROWS = BLOCKS * KM
SHARDS = 16
UNITS_DEV = ROWS // UNIT
OUT_UNITS = 3 * CAP + 1
BACK_UNITS = 3 * CAP + 2
RIM = KM + 3 * UNIT


def call(kernel, out_shape, scratch, *operands, scalars=0):
    return pl.pallas_call(
        kernel,
        out_shape=out_shape,
        in_specs=[SMEM] * scalars + [VMEM] * (len(operands) - scalars),
        out_specs=jax.tree.map(lambda _: VMEM, out_shape),
        scratch_shapes=scratch,
        interpret=INTERPRET,
    )(*operands)


def shape(*dims, dtype=BF16):
    return jax.ShapeDtypeStruct(dims, dtype)


def parts_of(value):
    high = value.astype(BF16).astype(F32)
    rest = value - high
    middle = rest.astype(BF16).astype(F32)
    return high, middle, rest - middle


def block_facts(records, tails, block):
    second = records[0]
    third = records[0] + records[1]
    end = third + records[2]

    def begins(index):
        return (index == 0) | (index == second) | (index == third)

    used = jnp.where(
        block + 1 == second,
        tails[0],
        jnp.where(block + 1 == third, tails[1], jnp.where(block + 1 == end, tails[2], KM)),
    )
    carry = jnp.where(begins(block), 0.0, 1.0).astype(F32)
    carry_next = jnp.where(begins(block + 1) | (block + 1 == end), 0.0, 1.0).astype(F32)
    return carry, carry_next, used


def live_column(used):
    rows = lax.broadcasted_iota(jnp.int32, (KM, LANES), 0)
    return (rows < used).astype(F32)


def fold8(value):
    return jnp.sum(value.reshape(-1, 8, LANES), axis=0)


def pack_kernel(slot, streams, filters, out):
    taps = filters[...]
    high, middle, low = parts_of(taps[:, KM:])
    lane = lax.broadcasted_iota(jnp.int32, (8, LANES), 1)
    small = jnp.where(
        lane < 32,
        high,
        jnp.where(
            lane < 64,
            pltpu.roll(middle, 32, 1),
            jnp.where(lane < 96, pltpu.roll(low, 64, 1), 0.0),
        ),
    )
    panel = jnp.concatenate([taps[:, :KM], small], axis=0).astype(BF16)

    def give(shard, carry):
        out[shard, pl.ds(3 * CAP * UNIT, UNIT), :] = panel
        return carry

    lax.fori_loop(0, SHARDS, give, 0)

    def move(unit, carry):
        to = slot[unit]
        shard = to // CAP
        rank = to % CAP
        for s in range(3):
            out[shard, pl.ds(pl.multiple_of((s * CAP + rank) * UNIT, UNIT), UNIT), :] = streams[
                s, pl.ds(pl.multiple_of(unit * UNIT, UNIT), UNIT), :
            ]
        return carry

    lax.fori_loop(0, UNITS_DEV, move, 0)


def unpack_kernel(slot, records, tails, position, arrived, packed, mixer, small, rim, turned):
    def move(unit, carry):
        at = slot[unit]
        shard = at // CAP
        rank = at % CAP
        for s in range(3):
            packed[s, pl.ds(pl.multiple_of(unit * UNIT, UNIT), UNIT), :] = arrived[
                shard, pl.ds(pl.multiple_of((s * CAP + rank) * UNIT, UNIT), UNIT), :
            ]
        return carry

    lax.fori_loop(0, UNITS_DEV, move, 0)
    for shard in range(SHARDS):
        panel = arrived[shard, 3 * CAP * UNIT :, :].astype(F32)
        turned[0, shard * 8 : shard * 8 + 8, :] = panel[:8]
        turned[1, shard * 8 : shard * 8 + 8, :] = panel[8:]
    mixer[...] = turned[0].T
    pieces = turned[1].T
    small[...] = pieces[0:32] + pieces[32:64] + pieces[64:96]

    _, _, used = block_facts(records, tails, position[0] * BLOCKS + BLOCKS - 1)
    live = live_column(used)
    both = []
    for s in (1, 2):
        wide = packed[s, ROWS - KM - UNIT :, :].astype(F32)
        total = jnp.zeros((KM, LANES), F32)
        for tap in range(KF):
            row = tap * 3 + s
            total = total + small[row : row + 1, :] * wide[UNIT - tap : UNIT - tap + KM]
        both.append((total * live).astype(BF16).astype(F32))
    rim[:KM, :] = (both[0] * both[1]).astype(BF16)
    carry, _, _ = block_facts(records, tails, position[0] * BLOCKS + BLOCKS - 1)

    @pl.when(carry == 0.0)
    def _():
        heads = []
        for s in (1, 2):
            wide = packed[s, ROWS - KM - UNIT : ROWS - KM + UNIT, :].astype(F32)
            rows = lax.broadcasted_iota(jnp.int32, (2 * UNIT, LANES), 0)
            wide = jnp.where(rows < UNIT, 0.0, wide)
            total = jnp.zeros((UNIT, LANES), F32)
            for tap in range(KF):
                row = tap * 3 + s
                total = total + small[row : row + 1, :] * wide[UNIT - tap : 2 * UNIT - tap]
            heads.append((total * live[:UNIT]).astype(BF16).astype(F32))
        rim[:UNIT, :] = (heads[0] * heads[1]).astype(BF16)

    for s in range(3):
        rim[KM + s * UNIT : KM + (s + 1) * UNIT, :] = packed[s, ROWS - UNIT :, :]


def forward_kernel(
    records,
    tails,
    position,
    packed,
    rim,
    mixer,
    small,
    out_grad,
    feature,
    response,
    sums,
    window,
    mixed,
    pair,
    shifted,
):
    first = position[0] * BLOCKS
    mixed[:KM, :] = rim[:KM, :].astype(F32)
    for b in range(BLOCKS):
        carry, _, used = block_facts(records, tails, first + b)
        live = live_column(used)
        both = []
        for s in range(3):
            if b == 0:
                tail = rim[KM + s * UNIT : KM + (s + 1) * UNIT, :].astype(F32)
            else:
                tail = packed[s, b * KM - UNIT : b * KM, :].astype(F32)
            window[s, :UNIT, :] = tail * carry
            window[s, UNIT:, :] = packed[s, b * KM : (b + 1) * KM, :].astype(F32)
            total = jnp.zeros((KM, LANES), F32)
            for tap in range(KF):
                row = tap * 3 + s
                total = total + small[row : row + 1, :] * window[s, UNIT - tap : UNIT - tap + KM, :]
            rounded = (total * live).astype(BF16)
            feature[s, b * KM : (b + 1) * KM, :] = rounded
            both.append(rounded.astype(F32))
        mixed[(b + 1) * KM : (b + 2) * KM, :] = (both[1] * both[2]).astype(BF16).astype(F32)

    gain = small[21:22, :]
    ones = jnp.ones((8, LANES), F32)
    line = lax.broadcasted_iota(jnp.int32, (8, LANES), 0)

    def one_block(b, collected):
        carry, _, _ = block_facts(records, tails, first + b)
        here = pl.ds(pl.multiple_of(b * KM, KM), KM)
        pair[:KM, :] = mixed[here, :] * carry
        pair[KM:, :] = mixed[pl.ds(pl.multiple_of((b + 1) * KM, KM), KM), :]
        for s in range(8):
            shifted[s, 8:, :] = pair[8 - s : 2 * KM - s, :]
        total = jnp.zeros((KM, LANES), F32)
        for s in range(8):
            for k in range(16):
                lag = 8 * k + s
                total = total + mixer[lag : lag + 1, :] * shifted[s, KM - 8 * k : 2 * KM - 8 * k, :]
        response[here, :] = total
        gated = (feature[0, here, :].astype(F32) * total).astype(BF16).astype(F32)
        weighted = out_grad[here, :].astype(F32) * gain
        contract = (((1,), (1,)), ((), ()))
        squares = lax.dot_general(
            ones, gated * gated, contract, precision=lax.Precision.HIGHEST,
            preferred_element_type=F32,
        )
        inner = lax.dot_general(
            ones, weighted * gated, contract, precision=lax.Precision.HIGHEST,
            preferred_element_type=F32,
        )
        return jnp.where(line == b, squares, jnp.where(line == b + BLOCKS, inner, collected))

    collected = lax.fori_loop(0, BLOCKS, one_block, jnp.zeros((8, LANES), F32))
    for member in range(sums.shape[0]):
        sums[member] = collected


def middle_kernel(
    records,
    tails,
    position,
    sums,
    feature,
    response,
    mixer,
    small,
    out_grad,
    out,
    query,
    reply,
    gain_sum,
    rim,
    window,
):
    first = position[0] * BLOCKS
    total = jnp.sum(sums[...], axis=0)
    line = lax.broadcasted_iota(jnp.int32, (8, LANES), 0)
    lane = lax.broadcasted_iota(jnp.int32, (8, LANES), 1)
    used = jnp.full((8, LANES), KM, jnp.int32)
    for b in range(BLOCKS):
        _, _, own = block_facts(records, tails, first + b)
        used = jnp.where(line == b, own, used)
    scale = (lane < used).astype(F32) * lax.rsqrt(total / C + EPSILON)
    inner = pltpu.roll(total, BLOCKS, 0) * scale / C
    both = jnp.where(line < BLOCKS, scale, pltpu.roll(inner, BLOCKS, 0))
    columns = jnp.concatenate([both] * 16, axis=0).T
    gain = small[21:22, :]
    gain_total = jnp.zeros((8, LANES), F32)
    for b in range(BLOCKS):
        here = slice(b * KM, (b + 1) * KM)
        scale_b = jnp.broadcast_to(columns[:, b : b + 1], (KM, LANES))
        inner_b = jnp.broadcast_to(columns[:, b + BLOCKS : b + BLOCKS + 1], (KM, LANES))
        query_feature = feature[0, here, :].astype(F32)
        answer = response[here, :]
        gated = (query_feature * answer).astype(BF16).astype(F32)
        normed = gated * scale_b
        out[here, :] = (normed * gain).astype(BF16)
        grad = out_grad[here, :].astype(F32)
        gain_total = gain_total + fold8(grad * normed)
        d_gated = (scale_b * (grad * gain - normed * inner_b)).astype(BF16).astype(F32)
        query[here, :] = (d_gated * answer).astype(BF16)
        reply[here, :] = (d_gated * query_feature).astype(BF16)
    gain_sum[...] = gain_total

    _, carry_next, _ = block_facts(records, tails, first)
    window[:KM, :] = reply[:KM, :].astype(F32)
    window[KM:, :] = reply[KM : KM + UNIT, :].astype(F32) * carry_next
    totals = [jnp.zeros((8, LANES), F32) for _ in range(4)]
    for lag in range(KM):
        totals[lag % 4] = totals[lag % 4] + mixer[lag : lag + 1, :] * window[lag : lag + 8, :]
    d_mixed = (totals[0] + totals[1]) + (totals[2] + totals[3])
    d_mixed = jnp.concatenate([d_mixed, jnp.zeros_like(d_mixed)], axis=0)
    rim[:KM, :] = reply[:KM, :]
    rim[KM : KM + UNIT, :] = query[:UNIT, :]
    rim[KM + UNIT : KM + 2 * UNIT, :] = (d_mixed * feature[2, :UNIT, :].astype(F32)).astype(BF16)
    rim[KM + 2 * UNIT :, :] = (d_mixed * feature[1, :UNIT, :].astype(F32)).astype(BF16)


def backward_kernel(
    slot,
    records,
    tails,
    position,
    query,
    reply,
    rim_back,
    feature,
    packed,
    rim,
    mixer,
    small,
    gain_sum,
    back,
    mixed,
    replies,
    pair,
    shifted,
    lag_total,
    d_feature,
    window,
    tap_total,
    spread,
):
    first = position[0] * BLOCKS
    mixed[:KM, :] = rim[:KM, :].astype(F32)
    replies[ROWS:, :] = rim_back[:KM, :].astype(F32)
    for b in range(BLOCKS):
        here = slice(b * KM, (b + 1) * KM)
        product = feature[1, here, :].astype(F32) * feature[2, here, :].astype(F32)
        mixed[(b + 1) * KM : (b + 2) * KM, :] = product.astype(BF16).astype(F32)
        replies[here, :] = reply[here, :].astype(F32)
    for s in range(3):
        d_feature[s, ROWS:, :] = rim_back[KM + s * UNIT : KM + (s + 1) * UNIT, :].astype(F32)
    d_feature[0, :ROWS, :] = query[...].astype(F32)
    lag_total[...] = jnp.zeros_like(lag_total)

    def one_block(b, unused):
        carry, carry_next, _ = block_facts(records, tails, first + b)
        here = pl.ds(pl.multiple_of(b * KM, KM), KM)
        after = pl.ds(pl.multiple_of((b + 1) * KM, KM), KM)
        pair[:KM, :] = replies[here, :]
        pair[KM:, :] = replies[after, :] * carry_next
        for s in range(8):
            shifted[s, : 2 * KM - 8, :] = pair[s : 2 * KM - 8 + s, :]
        total = jnp.zeros((KM, LANES), F32)
        for s in range(8):
            for k in range(16):
                lag = 8 * k + s
                total = total + mixer[lag : lag + 1, :] * shifted[s, 8 * k : 8 * k + KM, :]
        d_feature[1, here, :] = (total * feature[2, here, :].astype(F32)).astype(BF16).astype(F32)
        d_feature[2, here, :] = (total * feature[1, here, :].astype(F32)).astype(BF16).astype(F32)
        pair[:KM, :] = mixed[here, :] * carry
        pair[KM:, :] = mixed[after, :]
        for s in range(8):
            shifted[s, 8:, :] = pair[8 - s : 2 * KM - s, :]
        own = replies[here, :]
        for s in range(8):
            for k in range(16):
                lag = 8 * k + s
                lag_total[lag] = lag_total[lag] + fold8(
                    own * shifted[s, KM - 8 * k : 2 * KM - 8 * k, :]
                )
        return unused

    lax.fori_loop(0, BLOCKS, one_block, 0)

    tap_total[...] = jnp.zeros_like(tap_total)
    for b in range(BLOCKS):
        carry, carry_next, _ = block_facts(records, tails, first + b)
        here = slice(b * KM, (b + 1) * KM)
        for s in range(3):
            if b == 0:
                tail = rim[KM + s * UNIT : KM + (s + 1) * UNIT, :].astype(F32)
            else:
                tail = packed[s, b * KM - UNIT : b * KM, :].astype(F32)
            window[:UNIT, :] = tail * carry
            window[UNIT:, :] = packed[s, here, :].astype(F32)
            own = d_feature[s, here, :]
            for tap in range(KF):
                row = tap * 3 + s
                tap_total[row] = tap_total[row] + fold8(own * window[UNIT - tap : UNIT - tap + KM, :])
            window[:KM, :] = own
            window[KM:, :] = d_feature[s, (b + 1) * KM : (b + 1) * KM + UNIT, :] * carry_next
            total = jnp.zeros((KM, LANES), F32)
            for tap in range(KF):
                row = tap * 3 + s
                total = total + small[row : row + 1, :] * window[tap : tap + KM, :]
            spread[s, here, :] = total.astype(BF16)

    tap_total[21] = gain_sum[...]
    mixer_parts = parts_of(jnp.sum(lag_total[...], axis=1).T)
    small_parts = parts_of(jnp.sum(tap_total[...], axis=1))
    rest = jnp.zeros((KM - 96, LANES), F32)
    turned = jnp.concatenate(list(small_parts) + [rest], axis=0).T
    for shard in range(SHARDS):
        rows = slice(shard * 8, shard * 8 + 8)
        pieces = jnp.concatenate([part[rows] for part in mixer_parts] + [turned[rows]], axis=0)
        back[shard, 3 * CAP * UNIT :, :] = pieces.astype(BF16)

    def move(unit, carry):
        to = slot[unit]
        shard = to // CAP
        rank = to % CAP
        for s in range(3):
            back[shard, pl.ds(pl.multiple_of((s * CAP + rank) * UNIT, UNIT), UNIT), :] = spread[
                s, pl.ds(pl.multiple_of(unit * UNIT, UNIT), UNIT), :
            ]
        return carry

    lax.fori_loop(0, UNITS_DEV, move, 0)


def finish_kernel(slot, returned, stream_grad, grads):
    def move(unit, carry):
        at = slot[unit]
        shard = at // CAP
        rank = at % CAP
        for s in range(3):
            stream_grad[s, pl.ds(pl.multiple_of(unit * UNIT, UNIT), UNIT), :] = returned[
                shard, pl.ds(pl.multiple_of((s * CAP + rank) * UNIT, UNIT), UNIT), :
            ]
        return carry

    lax.fori_loop(0, UNITS_DEV, move, 0)
    total = jnp.zeros((2 * UNIT, LANES), F32)
    for shard in range(SHARDS):
        total = total + returned[shard, 3 * CAP * UNIT :, :].astype(F32)
    grads[:, :KM] = total[0:8] + total[8:16] + total[16:24]
    pieces = total[24:32]
    grads[:, KM:] = pieces + pltpu.roll(pieces, LANES - 32, 1) + pltpu.roll(pieces, LANES - 64, 1)


def routing(unit_dest, position):
    target = (unit_dest // UNITS_DEV).reshape(SHARDS, UNITS_DEV)
    ids = jnp.arange(UNITS_DEV, dtype=jnp.int32)
    same = (target[:, :, None] == target[:, None, :]) & (ids[None, :] < ids[:, None])[None]
    rank = jnp.sum(same.astype(jnp.int32), axis=2)
    own_slot = lax.dynamic_index_in_dim(target * CAP + rank, position, 0, keepdims=False)
    arrive = (jnp.arange(SHARDS, dtype=jnp.int32)[:, None] * CAP + rank).reshape(-1)
    match = unit_dest[None, :] == (position * UNITS_DEV + ids)[:, None]
    packed_slot = jnp.sum(jnp.where(match, arrive[None, :], 0), axis=1)
    return own_slot.astype(jnp.int32), packed_slot.astype(jnp.int32)


def body(
    streams, record_blocks, tail_rows, unit_dest, mixer_filter, feat_filter, norm_gain, out_grad
):
    members = lax.axis_size("fsdp")
    position = lax.axis_index("seq").astype(jnp.int32)
    own_slot, packed_slot = routing(unit_dest, position)
    where = position.reshape(1)
    filters = jnp.concatenate(
        [
            mixer_filter,
            feat_filter.reshape(KF * 3, 8),
            norm_gain.reshape(1, 8),
            jnp.zeros((LANES - KF * 3 - 1, 8), F32),
        ],
        axis=0,
    ).T
    outgoing = call(
        pack_kernel,
        shape(SHARDS, OUT_UNITS * UNIT, LANES),
        [],
        own_slot,
        streams,
        filters,
        scalars=1,
    )
    arrived = lax.all_to_all(outgoing, "seq", split_axis=0, concat_axis=0, tiled=True)
    facts = (record_blocks, tail_rows, where)
    packed, mixer, small, rim_out = call(
        unpack_kernel,
        (
            shape(3, ROWS, LANES),
            shape(KM, LANES, dtype=F32),
            shape(32, LANES, dtype=F32),
            shape(RIM, LANES),
        ),
        [pltpu.VMEM((2, LANES, LANES), F32)],
        packed_slot,
        *facts,
        arrived,
        scalars=4,
    )
    rim = lax.ppermute(rim_out, "seq", [(i, i + 1) for i in range(SHARDS - 1)])
    feature, response, sums = call(
        forward_kernel,
        (
            shape(3, ROWS, LANES),
            shape(ROWS, LANES, dtype=F32),
            shape(members, 8, LANES, dtype=F32),
        ),
        [
            pltpu.VMEM((3, UNIT + KM, LANES), F32),
            pltpu.VMEM((ROWS + KM, LANES), F32),
            pltpu.VMEM((2 * KM, LANES), F32),
            pltpu.VMEM((8, 2 * KM, LANES), F32),
        ],
        *facts,
        packed,
        rim,
        mixer,
        small,
        out_grad,
        scalars=3,
    )
    sums = lax.all_to_all(sums, "fsdp", split_axis=0, concat_axis=0, tiled=True)
    out, query, reply, gain_sum, rim_back_out = call(
        middle_kernel,
        (
            shape(ROWS, LANES),
            shape(ROWS, LANES),
            shape(ROWS, LANES),
            shape(8, LANES, dtype=F32),
            shape(RIM, LANES),
        ),
        [pltpu.VMEM((KM + UNIT, LANES), F32)],
        *facts,
        sums,
        feature,
        response,
        mixer,
        small,
        out_grad,
        scalars=3,
    )
    rim_back = lax.ppermute(rim_back_out, "seq", [(i + 1, i) for i in range(SHARDS - 1)])
    returning = call(
        backward_kernel,
        shape(SHARDS, BACK_UNITS * UNIT, LANES),
        [
            pltpu.VMEM((ROWS + KM, LANES), F32),
            pltpu.VMEM((ROWS + KM, LANES), F32),
            pltpu.VMEM((2 * KM, LANES), F32),
            pltpu.VMEM((8, 2 * KM, LANES), F32),
            pltpu.VMEM((KM, 8, LANES), F32),
            pltpu.VMEM((3, ROWS + UNIT, LANES), F32),
            pltpu.VMEM((KM + UNIT, LANES), F32),
            pltpu.VMEM((32, 8, LANES), F32),
            pltpu.VMEM((3, ROWS, LANES), BF16),
        ],
        packed_slot,
        *facts,
        query,
        reply,
        rim_back,
        feature,
        packed,
        rim,
        mixer,
        small,
        gain_sum,
        scalars=4,
    )
    returned = lax.all_to_all(returning, "seq", split_axis=0, concat_axis=0, tiled=True)
    stream_grad, grads = call(
        finish_kernel,
        (shape(3, ROWS, LANES), shape(8, 2 * LANES, dtype=F32)),
        [],
        own_slot,
        returned,
        scalars=1,
    )
    turned = grads.T
    mixer_grad = turned[:KM]
    feat_grad = turned[KM : KM + KF * 3].reshape(KF, 3, 8)
    gain_grad = turned[KM + KF * 3]
    return (out, stream_grad, mixer_grad, feat_grad, gain_grad)


def solution(mesh):
    placed = (
        P(None, "seq", "fsdp"),
        P(),
        P(),
        P(),
        P(None, ("fsdp", "seq")),
        P(None, None, ("fsdp", "seq")),
        P(("fsdp", "seq")),
        P("seq", "fsdp"),
    )
    return jax.shard_map(
        body,
        mesh=mesh,
        in_specs=placed,
        out_specs=(
            P("seq", "fsdp"),
            P(None, "seq", "fsdp"),
            P(None, ("fsdp", "seq")),
            P(None, None, ("fsdp", "seq")),
            P(("fsdp", "seq")),
        ),
        check_vma=False,
    )
```

time: 797 us -> 155 us (0.19)
  blocking collectives: 399 us -> 58.1 us
  local copies, waits for them, and re-layouts: 195 us -> 5.97 us
  other arithmetic: 44.4 us -> 2.47 us
  starting transfers between devices: 53.5 us -> 19.5 us
  Pallas kernels: 0 us -> 25 us
  waiting for transfers between devices: 67 us -> 42.5 us
  matrix products: 19 us -> 0 us
  between operations: 16.1 us -> 0.73 us
    psum x3 -> x0, blocking collectives: 233 us -> none  [the longest x1 104 us: body(): lax.psum((mixer_term, feat_term, gain_term), 'seq')]
    gather x6 -> x0, local copies, waits for them, and re-layouts: 130 us -> none  [the longest x2 126 us: toeplitz(): return jnp.take(padded, jnp.asarray(lag_table(filter_bf.shape[0])), axis=1)]
    all_gather x2 -> x0, blocking collectives: 115 us -> none  [the longest x1 67.7 us: body(): lax.all_gather(feat_filter, 'seq', axis=2, tiled=True)]
    psum x1 -> x0, waiting for transfers between devices: 59.1 us -> none  [body(): lax.psum((mixer_term, feat_term, gain_term), 'seq')]
    all_to_all x0 -> x2, blocking collectives: none -> 58.1 us  [the longest x1 43.3 us: body(): lax.all_to_all(returning, 'seq', split_axis=0, concat_axis=0, tiled=True)]
    unnamed x1 -> x0, blocking collectives: 49.9 us -> none
    reshape x8 -> x4, local copies, waits for them, and re-layouts: 34 us -> 0.19 us  [the longest x2 0.09 us: body(): feat_filter.reshape(KF * 3, 8)]
    all_to_all x2 -> x1, waiting for transfers between devices: 0.01 us -> 30.6 us  [body(): lax.all_to_all(outgoing, 'seq', split_axis=0, concat_axis=0, tiled=True)]
  transfers between devices with their start and end apart: 7 -> 3, of which waited for: 2 -> 3; matrix products, arithmetic and copies ran while one was open for 29% -> 1% of each run, Pallas kernels for 0% -> 0%
where the time goes in v1:
time: 155 us; the launch traced here: 154 us
  blocking collectives  58.1 us (37%)
  waiting for transfers between devices  42.5 us (27%)
  Pallas kernels  25 us (16%)
  starting transfers between devices  19.5 us (13%)
  local copies, waits for them, and re-layouts  5.97 us (4%)
  other arithmetic  2.47 us (2%)
    all_to_all x1, blocking collectives, body(): lax.all_to_all(returning, 'seq', split_axis=0, concat_axis=0, tiled=True)  43.3 us
    all_to_all x1, waiting for transfers between devices, body(): lax.all_to_all(outgoing, 'seq', split_axis=0, concat_axis=0, tiled=True)  30.6 us
    pallas_call x6, Pallas kernels, call(): pl.pallas_call(kernel, out_shape=out_shape, in_specs=[SMEM] * scalars + [...  25 us
    all_to_all x1, starting transfers between devices, body(): lax.all_to_all(outgoing, 'seq', split_axis=0, concat_axis=0, tiled=True)  15.6 us
    all_to_all x1, blocking collectives, body(): sums = lax.all_to_all(sums, 'fsdp', split_axis=0, concat_axis=0, tiled=True)  14.8 us
    ppermute x1, waiting for transfers between devices, body(): lax.ppermute(rim_back_out, 'seq', [(i + 1, i) for i in range(SHARDS - 1)])  9.97 us
    unnamed x18, local copies, waits for them, and re-layouts  3.42 us
  transfers between devices with their start and end apart: 3, of which 3 were waited for; matrix products, arithmetic and copies ran while one was open for 1% of the time, Pallas kernels for 0%

profile of v1, /device:TPU:2, one launch (start us, length us, event | category | flops | bytes accessed | tf_op | source)
XLA Modules:
  0.0 154.3 jit_solution(10401194906460003175)
XLA Ops:
  0.7 0.6 copy-done.5
  1.4 0.1 copy.23
  1.4 0.1 eq.31
  1.5 0.1 copy.22
  1.6 0.1 pad.3.clone
  1.7 0.5 convert_reduce_fusion
  2.2 0.5 fusion.2.slot
  2.7 0.7 maximum_bitcast_fusion.filters
  3.4 2.6 %shard_map.119 = bf16[16,208,128]{2,1,0:T(8,128)(2,1)} custom-call(s32[32]{0:T(128)} %fusion.2.slot, bf16[3,512,128]{2,1,0:T(8,128)(2,1)} %streams.1, f32[8,256]{1,0:T(8,128)} %maximum_bitcast_fusion.filters), custom_call_target="tpu_custom_call" | custom-call | tf_op jit(solution)/shard_map/pallas_call | solution.py:34
  5.9 15.6 %all-to-all-start = ((bf16[16,208,128]{2,1,0:T(8,128)(2,1)}), bf16[16,208,128]{2,1,0:T(8,128)(2,1)S(1)}, u32[]{:S(2)}, u32[]{:S(2)}) async-start(bf16[16,208,128]{2,1,0:T(8,128)(2,1)} %shard_map.119), calls=%async_computation | async-start | bytes 1703936 | tf_op jit(solution)/shard_map/all_to_all | solution.py:473
  21.6 0.1 broadcast_add_fusion
  21.7 0.1 add.37
  21.8 0.7 select_reduce_fusion.slot
  22.5 30.6 %all-to-all-done.arrived = bf16[16,208,128]{2,1,0:T(8,128)(2,1)S(1)} async-done(((bf16[16,208,128]{2,1,0:T(8,128)(2,1)}), bf16[16,208,128]{2,1,0:T(8,128)(2,1)S(1)}, u32[]{:S(2)}, u32[]{:S(2)}) %all-to-all-start) | async-done | bytes 852000 | tf_op jit(solution)/shard_map/all_to_all | solution.py:473
  53.0 0.9 copy-done
  53.9 2.7 %shard_map.120 = (bf16[3,512,128]{2,1,0:T(8,128)(2,1)}, f32[128,128]{1,0:T(8,128)}, f32[32,128]{1,0:T(8,128)}, bf16[176,128]{1,0:T(8,128)(2,1)}) custom-call(s32[32]{0:T(128)} %select_reduce_fusion.slot, s32[3]{0:T(128)} %records.7, s32[3]{0:T(128)} %tails.7, s32[1]{0:T(128)} %bitcast.position, bf16[16,208,128]{2,1,0:T(8,128)(2,1)} %copy-done), custom_call_target="tpu_custom_call" | custom-call | tf_op jit(solution)/shard_map/pallas_call | solution.py:34
  56.6 2.5 %collective-permute-start = (bf16[176,128]{1,0:T(8,128)(2,1)}, bf16[176,128]{1,0:T(8,128)(2,1)S(1)}, u32[]{:S(2)}, u32[]{:S(2)}) collective-permute-start(bf16[176,128]{1,0:T(8,128)(2,1)} %get-tuple-element.20), channel_id=1, source_target_pairs={{0,1},{1,2},{2,3},{3,4},{4,5},{5,6},{6,7},{7,8},{8,9},{9,10},{10,1... | collective-permute-start | bytes 135176 | tf_op jit(solution)/shard_map/ppermute | solution.py:489
  59.2 2.0 %collective-permute-done.rim = bf16[176,128]{1,0:T(8,128)(2,1)S(1)} collective-permute-done((bf16[176,128]{1,0:T(8,128)(2,1)}, bf16[176,128]{1,0:T(8,128)(2,1)S(1)}, u32[]{:S(2)}, u32[]{:S(2)}) %collective-permute-start) | collective-permute-done | bytes 45088 | tf_op jit(solution)/shard_map/ppermute | solution.py:489
  61.2 0.6 copy-done.1
  61.8 6.0 %shard_map.121 = (bf16[3,512,128]{2,1,0:T(8,128)(2,1)}, f32[512,128]{1,0:T(8,128)}, f32[32,8,128]{2,1,0:T(8,128)}) custom-call(s32[3]{0:T(128)} %records.7, s32[3]{0:T(128)} %tails.7, s32[1]{0:T(128)} %bitcast.position, bf16[3,512,128]{2,1,0:T(8,128)(2,1)} %get-tuple-element.19.packed, bf16[176,128]{1,0:T(8,128)(2,1)} %copy-done.1, ...), custom_call_target="tpu_custom_call" | custom-call | tf_op jit(solution)/shard_map/pallas_call | solution.py:34
  67.8 14.8 %all_to_all.15.sums = f32[32,8,128]{2,1,0:T(8,128)} all-to-all(f32[32,8,128]{2,1,0:T(8,128)} %get-tuple-element.23), channel_id=1, replica_groups=mesh['fsdp'=32,'seq'=16] {'fsdp'}, dimensions={0} | all-to-all | bytes 262144 | tf_op jit(solution)/shard_map/all_to_all | solution.py:511
  82.6 2.4 %shard_map.122 = (bf16[512,128]{1,0:T(8,128)(2,1)}, bf16[512,128]{1,0:T(8,128)(2,1)}, bf16[512,128]{1,0:T(8,128)(2,1)}, f32[8,128]{1,0:T(8,128)}, bf16[176,128]{1,0:T(8,128)(2,1)}) custom-call(s32[3]{0:T(128)} %records.7, s32[3]{0:T(128)} %tails.7, s32[1]{0:T(128)} %bitcast.position, f32[32,8,128]{2,1,0:T(8,128)} %all_to_all.15.sums, ...), custom_call_target="tpu_custom_call" | custom-call | tf_op jit(solution)/shard_map/pallas_call | solution.py:34
  85.0 1.3 collective-permute-start.1
  86.3 10.0 %collective-permute-done.1.rim_back = bf16[176,128]{1,0:T(8,128)(2,1)S(1)} collective-permute-done((bf16[176,128]{1,0:T(8,128)(2,1)}, bf16[176,128]{1,0:T(8,128)(2,1)S(1)}, u32[]{:S(2)}, u32[]{:S(2)}) %collective-permute-start.1) | collective-permute-done | bytes 45088 | tf_op jit(solution)/shard_map/ppermute | solution.py:531
  96.2 0.6 copy-done.2
  96.9 8.9 %shard_map.123 = bf16[16,224,128]{2,1,0:T(8,128)(2,1)} custom-call(s32[32]{0:T(128)} %select_reduce_fusion.slot, s32[3]{0:T(128)} %records.7, s32[3]{0:T(128)} %tails.7, s32[1]{0:T(128)} %bitcast.position, bf16[512,128]{1,0:T(8,128)(2,1)} %get-tuple-element.27.query, bf16[512,128]{1,0:T(8,128)(2,1)} %get-tuple-element.28.reply, bf16[176,128]{1,0:T(8,128)(2,1)} %copy-done.2, ...), custom_call_target="tpu_custom_call" | custom-call | tf_op jit(solution)/shard_map/pallas_call | solution.py:34
  105.8 43.3 %all_to_all.16.returned = bf16[16,224,128]{2,1,0:T(8,128)(2,1)} all-to-all(bf16[16,224,128]{2,1,0:T(8,128)(2,1)} %shard_map.123), channel_id=1, replica_groups=mesh['fsdp'=32,'seq'=16] {'seq'}, dimensions={0} | all-to-all | bytes 1835008 | tf_op jit(solution)/shard_map/all_to_all | solution.py:559
  149.1 2.5 %shard_map.124 = (bf16[3,512,128]{2,1,0:T(8,128)(2,1)}, f32[8,256]{1,0:T(8,128)}) custom-call(s32[32]{0:T(128)} %fusion.2.slot, bf16[16,224,128]{2,1,0:T(8,128)(2,1)} %all_to_all.16.returned), custom_call_target="tpu_custom_call" | custom-call | tf_op jit(solution)/shard_map/pallas_call | solution.py:34
  151.6 1.5 slice_reduce_fusion
  153.0 0.6 slice.12
  153.6 0.1 copy.24
  153.7 0.6 copy.25
  (21 shorter events, 0.1 us)
Async XLA Ops:
  0.7 0.7 copy-start.5
  0.7 0.7 copy-start.7
  0.7 0.8 copy-start.4
  1.7 1.0 copy-start.6
  5.9 47.1 %all-to-all-start = ((bf16[16,208,128]{2,1,0:T(8,128)(2,1)}), bf16[16,208,128]{2,1,0:T(8,128)(2,1)S(1)}, u32[]{:S(2)}, u32[]{:S(2)}) async-start(bf16[16,208,128]{2,1,0:T(8,128)(2,1)} %shard_map.119), calls=%async_computation | async-start | bytes 1703936 | tf_op jit(solution)/shard_map/all_to_all | solution.py:473
  53.0 0.9 copy-start
  56.6 4.5 %collective-permute-start = (bf16[176,128]{1,0:T(8,128)(2,1)}, bf16[176,128]{1,0:T(8,128)(2,1)S(1)}, u32[]{:S(2)}, u32[]{:S(2)}) collective-permute-start(bf16[176,128]{1,0:T(8,128)(2,1)} %get-tuple-element.20), channel_id=1, source_target_pairs={{0,1},{1,2},{2,3},{3,4},{4,5},{5,6},{6,7},{7,8},{8,9},{9,10},{10,1... | collective-permute-start | bytes 135176 | tf_op jit(solution)/shard_map/ppermute | solution.py:489
  61.2 0.6 copy-start.1
  85.0 11.3 %collective-permute-start.1 = (bf16[176,128]{1,0:T(8,128)(2,1)}, bf16[176,128]{1,0:T(8,128)(2,1)S(1)}, u32[]{:S(2)}, u32[]{:S(2)}) collective-permute-start(bf16[176,128]{1,0:T(8,128)(2,1)} %get-tuple-element.29), channel_id=1, source_target_pairs={{1,0},{2,1},{3,2},{4,3},{5,4},{6,5},{7,6},{8,7},{9,8},{10,9},{11,1... | collective-permute-start | bytes 135176 | tf_op jit(solution)/shard_map/ppermute | solution.py:531
  96.2 0.6 copy-start.2
  151.6 1.5 copy-start.3

commit v2 on v1

--- a/solution.py
+++ b/solution.py
@@ -234,8 +234,7 @@
         return jnp.where(line == b, squares, jnp.where(line == b + BLOCKS, inner, collected))
 
     collected = lax.fori_loop(0, BLOCKS, one_block, jnp.zeros((8, LANES), F32))
-    for member in range(sums.shape[0]):
-        sums[member] = collected
+    sums[...] = collected
 
 
 def middle_kernel(
@@ -432,6 +431,118 @@
     pieces = total[24:32]
     grads[:, KM:] = pieces + pltpu.roll(pieces, LANES - 32, 1) + pltpu.roll(pieces, LANES - 64, 1)
 
+MESH = pl.DeviceIdType.MESH
+
+
+def remote_call(kernel, out_shape, scratch, collective, *operands):
+    return pl.pallas_call(
+        kernel,
+        out_shape=out_shape,
+        in_specs=[VMEM] * len(operands),
+        out_specs=VMEM,
+        scratch_shapes=scratch,
+        compiler_params=pltpu.CompilerParams(collective_id=collective, has_side_effects=True),
+    )(*operands)
+
+
+def exchange_kernel(blocks, out, sent, came, own):
+    member = lax.axis_index("fsdp")
+    me = lax.axis_index("seq")
+    row, half = me // 2, me % 2
+    peers = []
+    for away in (1, 7, 2, 6, 3, 5, 4):
+        peers.append((away, half))
+        peers.append((away, 1 - half))
+    peers.append((0, 1 - half))
+    barrier = pltpu.get_barrier_semaphore()
+    for away, side in peers:
+        to = (row + away) % 8 * 2 + side
+        pl.semaphore_signal(barrier, inc=1, device_id=(member, to), device_id_type=MESH)
+    pl.semaphore_wait(barrier, len(peers))
+    mine = pltpu.make_async_copy(blocks.at[me], out.at[me], own)
+    mine.start()
+    copies = []
+    for number, (away, side) in enumerate(peers):
+        to = (row + away) % 8 * 2 + side
+        copy = pltpu.make_async_remote_copy(
+            src_ref=blocks.at[to],
+            dst_ref=out.at[me],
+            send_sem=sent.at[number],
+            recv_sem=came.at[number],
+            device_id=(member, to),
+            device_id_type=MESH,
+        )
+        copy.start()
+        copies.append(copy)
+    mine.wait()
+    for copy in copies:
+        copy.wait_send()
+    for copy in copies:
+        copy.wait_recv()
+
+
+def exchange(blocks, collective):
+    if INTERPRET:
+        return lax.all_to_all(blocks, "seq", split_axis=0, concat_axis=0, tiled=True)
+    return remote_call(
+        exchange_kernel,
+        shape(*blocks.shape, dtype=blocks.dtype),
+        [
+            pltpu.SemaphoreType.DMA((SHARDS,)),
+            pltpu.SemaphoreType.DMA((SHARDS,)),
+            pltpu.SemaphoreType.DMA,
+        ],
+        collective,
+        blocks,
+    )
+
+
+def gather_kernel(value, out, sent, came, own):
+    members = out.shape[0]
+    member = lax.axis_index("fsdp")
+    me = lax.axis_index("seq")
+    barrier = pltpu.get_barrier_semaphore()
+    for away in range(1, members):
+        to = (member + away) % members
+        pl.semaphore_signal(barrier, inc=1, device_id=(to, me), device_id_type=MESH)
+    pl.semaphore_wait(barrier, members - 1)
+    mine = pltpu.make_async_copy(value, out.at[member], own)
+    mine.start()
+    copies = []
+    for away in range(1, members):
+        to = (member + away) % members
+        copy = pltpu.make_async_remote_copy(
+            src_ref=value,
+            dst_ref=out.at[member],
+            send_sem=sent.at[away],
+            recv_sem=came.at[away],
+            device_id=(to, me),
+            device_id_type=MESH,
+        )
+        copy.start()
+        copies.append(copy)
+    mine.wait()
+    for copy in copies:
+        copy.wait_send()
+    for copy in copies:
+        copy.wait_recv()
+
+
+def gather(value, members, collective):
+    if INTERPRET:
+        return lax.all_gather(value, "fsdp")
+    return remote_call(
+        gather_kernel,
+        shape(members, *value.shape, dtype=value.dtype),
+        [
+            pltpu.SemaphoreType.DMA((members,)),
+            pltpu.SemaphoreType.DMA((members,)),
+            pltpu.SemaphoreType.DMA,
+        ],
+        collective,
+        value,
+    )
+
 
 def routing(unit_dest, position):
     target = (unit_dest // UNITS_DEV).reshape(SHARDS, UNITS_DEV)
@@ -470,7 +581,7 @@
         filters,
         scalars=1,
     )
-    arrived = lax.all_to_all(outgoing, "seq", split_axis=0, concat_axis=0, tiled=True)
+    arrived = exchange(outgoing, 0)
     facts = (record_blocks, tail_rows, where)
     packed, mixer, small, rim_out = call(
         unpack_kernel,
@@ -492,7 +603,7 @@
         (
             shape(3, ROWS, LANES),
             shape(ROWS, LANES, dtype=F32),
-            shape(members, 8, LANES, dtype=F32),
+            shape(8, LANES, dtype=F32),
         ),
         [
             pltpu.VMEM((3, UNIT + KM, LANES), F32),
@@ -508,7 +619,7 @@
         out_grad,
         scalars=3,
     )
-    sums = lax.all_to_all(sums, "fsdp", split_axis=0, concat_axis=0, tiled=True)
+    sums = gather(sums, members, 1)
     out, query, reply, gain_sum, rim_back_out = call(
         middle_kernel,
         (
@@ -556,7 +667,7 @@
         gain_sum,
         scalars=4,
     )
-    returned = lax.all_to_all(returning, "seq", split_axis=0, concat_axis=0, tiled=True)
+    returned = exchange(returning, 2)
     stream_grad, grads = call(
         finish_kernel,
         (shape(3, ROWS, LANES), shape(8, 2 * LANES, dtype=F32)),

time: 155 us -> 140 us (0.903)
  the two profiles are of different devices: /device:TPU:2 before, /device:TPU:16 now
where the time goes in v2:
time: 140 us; the launch traced here: 139 us
  Pallas kernels  108 us (77%)
  starting transfers between devices  13.5 us (10%)
  waiting for transfers between devices  7.97 us (6%)
  local copies, waits for them, and re-layouts  6.78 us (5%)
  other arithmetic  2.41 us (2%)
    pallas_call x3, Pallas kernels, remote_call(): pl.pallas_call(kernel, out_shape=out_shape, in_specs=[VMEM] * len(operand...  83 us
    pallas_call x6, Pallas kernels, call(): pl.pallas_call(kernel, out_shape=out_shape, in_specs=[SMEM] * scalars + [...  25 us
    ppermute x1, starting transfers between devices, body(): rim = lax.ppermute(rim_out, 'seq', [(i, i + 1) for i in range(SHARDS - 1)])  7.24 us
    ppermute x1, starting transfers between devices, body(): lax.ppermute(rim_back_out, 'seq', [(i + 1, i) for i in range(SHARDS - 1)])  6.22 us
    unnamed x16, local copies, waits for them, and re-layouts  4.23 us
    ppermute x1, waiting for transfers between devices, body(): rim = lax.ppermute(rim_out, 'seq', [(i, i + 1) for i in range(SHARDS - 1)])  4.15 us
    ppermute x1, waiting for transfers between devices, body(): lax.ppermute(rim_back_out, 'seq', [(i + 1, i) for i in range(SHARDS - 1)])  3.82 us
  transfers between devices with their start and end apart: 2, of which 2 were waited for; matrix products, arithmetic and copies ran while one was open for 0% of the time, Pallas kernels for 0%

profile of v2, /device:TPU:16, one launch (start us, length us, event | category | flops | bytes accessed | tf_op | source)
XLA Modules:
  0.0 139.4 jit_solution(10834364007905379405)
XLA Ops:
  0.7 0.7 copy-done.4
  1.4 0.6 copy-done.6
  2.0 0.1 copy.23
  2.1 0.1 eq.31
  2.2 0.5 convert_reduce_fusion
  2.6 0.5 fusion.2.slot
  3.2 0.1 add.37
  3.3 0.6 copy-done.3
  3.9 0.1 copy.22
  3.9 0.1 pad.3.clone
  4.0 0.5 copy-done.5
  4.5 0.7 maximum_bitcast_fusion.filters
  5.2 2.6 %shard_map.119.blocks = bf16[16,208,128]{2,1,0:T(8,128)(2,1)} custom-call(s32[32]{0:T(128)} %fusion.2.slot, bf16[3,512,128]{2,1,0:T(8,128)(2,1)} %streams.1, f32[8,256]{1,0:T(8,128)} %maximum_bitcast_fusion.filters), custom_call_target="tpu_custom_call" | custom-call | tf_op jit(solution)/shard_map/pallas_call | solution.py:34
  7.8 36.9 %shard_map.120.arrived = bf16[16,208,128]{2,1,0:T(8,128)(2,1)} custom-call(bf16[16,208,128]{2,1,0:T(8,128)(2,1)} %shard_map.119.blocks), custom_call_target="tpu_custom_call" | custom-call | tf_op jit(solution)/shard_map/pallas_call | solution.py:438
  44.7 0.7 select_reduce_fusion.slot
  45.4 2.7 %shard_map.121 = (bf16[3,512,128]{2,1,0:T(8,128)(2,1)}, f32[128,128]{1,0:T(8,128)}, f32[32,128]{1,0:T(8,128)}, bf16[176,128]{1,0:T(8,128)(2,1)}) custom-call(s32[32]{0:T(128)} %select_reduce_fusion.slot, s32[3]{0:T(128)} %records.7, s32[3]{0:T(128)} %tails.7, s32[1]{0:T(128)} %bitcast.position, bf16[16,208,128]{2,1,0:T(8,128)(2,1)} %shard_map.120.arrived), custom_call_target="tpu_custom_call" | custom-call | tf_op jit(solution)/shard_map/pallas_call | solution.py:34
  48.1 7.2 %collective-permute-start = (bf16[176,128]{1,0:T(8,128)(2,1)}, bf16[176,128]{1,0:T(8,128)(2,1)S(1)}, u32[]{:S(2)}, u32[]{:S(2)}) collective-permute-start(bf16[176,128]{1,0:T(8,128)(2,1)} %get-tuple-element.20), channel_id=1, source_target_pairs={{0,1},{1,2},{2,3},{3,4},{4,5},{5,6},{6,7},{7,8},{8,9},{9,10},{10,1... | collective-permute-start | bytes 135176 | tf_op jit(solution)/shard_map/ppermute | solution.py:600
  55.4 4.2 %collective-permute-done.rim = bf16[176,128]{1,0:T(8,128)(2,1)S(1)} collective-permute-done((bf16[176,128]{1,0:T(8,128)(2,1)}, bf16[176,128]{1,0:T(8,128)(2,1)S(1)}, u32[]{:S(2)}, u32[]{:S(2)}) %collective-permute-start) | collective-permute-done | bytes 45088 | tf_op jit(solution)/shard_map/ppermute | solution.py:600
  59.5 0.6 copy-done
  60.1 6.0 %shard_map.122 = (bf16[3,512,128]{2,1,0:T(8,128)(2,1)}, f32[512,128]{1,0:T(8,128)}, f32[8,128]{1,0:T(8,128)}) custom-call(s32[3]{0:T(128)} %records.7, s32[3]{0:T(128)} %tails.7, s32[1]{0:T(128)} %bitcast.position, bf16[3,512,128]{2,1,0:T(8,128)(2,1)} %get-tuple-element.19.packed, bf16[176,128]{1,0:T(8,128)(2,1)} %copy-done, ...), custom_call_target="tpu_custom_call" | custom-call | tf_op jit(solution)/shard_map/pallas_call | solution.py:34
  66.1 11.4 %shard_map.123.sums = f32[32,8,128]{2,1,0:T(8,128)} custom-call(f32[8,128]{1,0:T(8,128)} %get-tuple-element.23.value), custom_call_target="tpu_custom_call" | custom-call | tf_op jit(solution)/shard_map/pallas_call | solution.py:438
  77.5 2.4 %shard_map.124 = (bf16[512,128]{1,0:T(8,128)(2,1)}, bf16[512,128]{1,0:T(8,128)(2,1)}, bf16[512,128]{1,0:T(8,128)(2,1)}, f32[8,128]{1,0:T(8,128)}, bf16[176,128]{1,0:T(8,128)(2,1)}) custom-call(s32[3]{0:T(128)} %records.7, s32[3]{0:T(128)} %tails.7, s32[1]{0:T(128)} %bitcast.position, f32[32,8,128]{2,1,0:T(8,128)} %shard_map.123.sums, ...), custom_call_target="tpu_custom_call" | custom-call | tf_op jit(solution)/shard_map/pallas_call | solution.py:34
  79.9 6.2 %collective-permute-start.1 = (bf16[176,128]{1,0:T(8,128)(2,1)}, bf16[176,128]{1,0:T(8,128)(2,1)S(1)}, u32[]{:S(2)}, u32[]{:S(2)}) collective-permute-start(bf16[176,128]{1,0:T(8,128)(2,1)} %get-tuple-element.29), channel_id=1, source_target_pairs={{1,0},{2,1},{3,2},{4,3},{5,4},{6,5},{7,6},{8,7},{9,8},{10,9},{11,1... | collective-permute-start | bytes 135176 | tf_op jit(solution)/shard_map/ppermute | solution.py:642
  86.1 3.8 %collective-permute-done.1.rim_back = bf16[176,128]{1,0:T(8,128)(2,1)S(1)} collective-permute-done((bf16[176,128]{1,0:T(8,128)(2,1)}, bf16[176,128]{1,0:T(8,128)(2,1)S(1)}, u32[]{:S(2)}, u32[]{:S(2)}) %collective-permute-start.1) | collective-permute-done | bytes 45088 | tf_op jit(solution)/shard_map/ppermute | solution.py:642
  89.9 0.6 copy-done.1
  90.6 8.9 %shard_map.125.blocks = bf16[16,224,128]{2,1,0:T(8,128)(2,1)} custom-call(s32[32]{0:T(128)} %select_reduce_fusion.slot, s32[3]{0:T(128)} %records.7, s32[3]{0:T(128)} %tails.7, s32[1]{0:T(128)} %bitcast.position, bf16[512,128]{1,0:T(8,128)(2,1)} %get-tuple-element.27.query, bf16[512,128]{1,0:T(8,128)(2,1)} %get-tuple-element.28.reply, ...), custom_call_target="tpu_custom_call" | custom-call | tf_op jit(solution)/shard_map/pallas_call | solution.py:34
  99.5 34.7 %shard_map.126.returned = bf16[16,224,128]{2,1,0:T(8,128)(2,1)} custom-call(bf16[16,224,128]{2,1,0:T(8,128)(2,1)} %shard_map.125.blocks), custom_call_target="tpu_custom_call" | custom-call | tf_op jit(solution)/shard_map/pallas_call | solution.py:438
  134.2 2.5 %shard_map.127 = (bf16[3,512,128]{2,1,0:T(8,128)(2,1)}, f32[8,256]{1,0:T(8,128)}) custom-call(s32[32]{0:T(128)} %fusion.2.slot, bf16[16,224,128]{2,1,0:T(8,128)(2,1)} %shard_map.126.returned), custom_call_target="tpu_custom_call" | custom-call | tf_op jit(solution)/shard_map/pallas_call | solution.py:34
  136.6 1.5 %slice_reduce_fusion = f32[8]{0:T(128)} fusion(f32[256,8]{0,1:T(8,128)} %bitcast.7), kind=kLoop, calls=%fused_computation.4 | loop fusion | bytes 64 | tf_op jit(solution)/shard_map/slice | solution.py:682
  138.1 0.6 slice.12
  138.7 0.1 copy.24
  138.8 0.6 copy.25
  (18 shorter events, 0.1 us)
Async XLA Ops:
  0.7 0.7 copy-start.4
  1.4 0.7 copy-start.6
  3.1 0.7 copy-start.3
  3.8 0.7 copy-start.5
  48.1 11.4 %collective-permute-start = (bf16[176,128]{1,0:T(8,128)(2,1)}, bf16[176,128]{1,0:T(8,128)(2,1)S(1)}, u32[]{:S(2)}, u32[]{:S(2)}) collective-permute-start(bf16[176,128]{1,0:T(8,128)(2,1)} %get-tuple-element.20), channel_id=1, source_target_pairs={{0,1},{1,2},{2,3},{3,4},{4,5},{5,6},{6,7},{7,8},{8,9},{9,10},{10,1... | collective-permute-start | bytes 135176 | tf_op jit(solution)/shard_map/ppermute | solution.py:600
  59.5 0.6 copy-start
  79.9 10.0 %collective-permute-start.1 = (bf16[176,128]{1,0:T(8,128)(2,1)}, bf16[176,128]{1,0:T(8,128)(2,1)S(1)}, u32[]{:S(2)}, u32[]{:S(2)}) collective-permute-start(bf16[176,128]{1,0:T(8,128)(2,1)} %get-tuple-element.29), channel_id=1, source_target_pairs={{1,0},{2,1},{3,2},{4,3},{5,4},{6,5},{7,6},{8,7},{9,8},{10,9},{11,1... | collective-permute-start | bytes 135176 | tf_op jit(solution)/shard_map/ppermute | solution.py:642
  89.9 0.6 copy-start.1
  136.6 1.5 %copy-start.2 = (f32[8,256]{1,0:T(8,128)S(1)}, f32[8,256]{1,0:T(8,128)}, u32[]{:S(2)}) copy-start(f32[8,256]{1,0:T(8,128)} %get-tuple-element.32) | copy-start | bytes 24580

commit v3 on v1

--- a/solution.py
+++ b/solution.py
@@ -70,16 +70,36 @@
     return carry, carry_next, used
 
 
-def live_column(used):
-    rows = lax.broadcasted_iota(jnp.int32, (KM, LANES), 0)
-    return (rows < used).astype(F32)
+def write_facts(facts, records, tails, first):
+    line = lax.broadcasted_iota(jnp.int32, (16, LANES), 0)
+    rows = jnp.zeros((16, LANES), F32)
+    for b in range(BLOCKS):
+        carry, carry_next, used = block_facts(records, tails, first + b)
+        rows = jnp.where(line == b, carry, rows)
+        rows = jnp.where(line == b + BLOCKS, carry_next, rows)
+        rows = jnp.where(line == b + 2 * BLOCKS, used.astype(F32), rows)
+    facts[...] = rows
+
+
+def carry_of(facts, b):
+    return facts[pl.ds(b, 1), :]
+
+
+def carry_next_of(facts, b):
+    return facts[pl.ds(b + BLOCKS, 1), :]
+
+
+def live_of(facts, b):
+    rows = lax.broadcasted_iota(jnp.int32, (KM, LANES), 0).astype(F32)
+    return jnp.where(rows < facts[pl.ds(b + 2 * BLOCKS, 1), :], 1.0, 0.0)
 
 
 def fold8(value):
     return jnp.sum(value.reshape(-1, 8, LANES), axis=0)
 
 
-def pack_kernel(slot, streams, filters, out):
+def pack_kernel(slot, records, tails, position, streams, filters, out, facts):
+    write_facts(facts, records, tails, position[0] * BLOCKS)
     taps = filters[...]
     high, middle, low = parts_of(taps[:, KM:])
     lane = lax.broadcasted_iota(jnp.int32, (8, LANES), 1)
@@ -113,7 +133,7 @@
     lax.fori_loop(0, UNITS_DEV, move, 0)
 
 
-def unpack_kernel(slot, records, tails, position, arrived, packed, mixer, small, rim, turned):
+def unpack_kernel(slot, facts, arrived, packed, mixer, small, rim, turned):
     def move(unit, carry):
         at = slot[unit]
         shard = at // CAP
@@ -133,41 +153,25 @@
     pieces = turned[1].T
     small[...] = pieces[0:32] + pieces[32:64] + pieces[64:96]
 
-    _, _, used = block_facts(records, tails, position[0] * BLOCKS + BLOCKS - 1)
-    live = live_column(used)
+    carry = carry_of(facts, BLOCKS - 1)
+    live = live_of(facts, BLOCKS - 1)
+    heads = lax.broadcasted_iota(jnp.int32, (KM + UNIT, LANES), 0) < UNIT
+    keep = jnp.where(heads, carry, 1.0)
     both = []
     for s in (1, 2):
-        wide = packed[s, ROWS - KM - UNIT :, :].astype(F32)
+        wide = packed[s, ROWS - KM - UNIT :, :].astype(F32) * keep
         total = jnp.zeros((KM, LANES), F32)
         for tap in range(KF):
             row = tap * 3 + s
             total = total + small[row : row + 1, :] * wide[UNIT - tap : UNIT - tap + KM]
         both.append((total * live).astype(BF16).astype(F32))
     rim[:KM, :] = (both[0] * both[1]).astype(BF16)
-    carry, _, _ = block_facts(records, tails, position[0] * BLOCKS + BLOCKS - 1)
-
-    @pl.when(carry == 0.0)
-    def _():
-        heads = []
-        for s in (1, 2):
-            wide = packed[s, ROWS - KM - UNIT : ROWS - KM + UNIT, :].astype(F32)
-            rows = lax.broadcasted_iota(jnp.int32, (2 * UNIT, LANES), 0)
-            wide = jnp.where(rows < UNIT, 0.0, wide)
-            total = jnp.zeros((UNIT, LANES), F32)
-            for tap in range(KF):
-                row = tap * 3 + s
-                total = total + small[row : row + 1, :] * wide[UNIT - tap : 2 * UNIT - tap]
-            heads.append((total * live[:UNIT]).astype(BF16).astype(F32))
-        rim[:UNIT, :] = (heads[0] * heads[1]).astype(BF16)
-
     for s in range(3):
         rim[KM + s * UNIT : KM + (s + 1) * UNIT, :] = packed[s, ROWS - UNIT :, :]
 
 
 def forward_kernel(
-    records,
-    tails,
-    position,
+    facts,
     packed,
     rim,
     mixer,
@@ -181,11 +185,10 @@
     pair,
     shifted,
 ):
-    first = position[0] * BLOCKS
     mixed[:KM, :] = rim[:KM, :].astype(F32)
     for b in range(BLOCKS):
-        carry, _, used = block_facts(records, tails, first + b)
-        live = live_column(used)
+        carry = carry_of(facts, b)
+        live = live_of(facts, b)
         both = []
         for s in range(3):
             if b == 0:
@@ -208,7 +211,7 @@
     line = lax.broadcasted_iota(jnp.int32, (8, LANES), 0)
 
     def one_block(b, collected):
-        carry, _, _ = block_facts(records, tails, first + b)
+        carry = carry_of(facts, b)
         here = pl.ds(pl.multiple_of(b * KM, KM), KM)
         pair[:KM, :] = mixed[here, :] * carry
         pair[KM:, :] = mixed[pl.ds(pl.multiple_of((b + 1) * KM, KM), KM), :]
@@ -234,14 +237,11 @@
         return jnp.where(line == b, squares, jnp.where(line == b + BLOCKS, inner, collected))
 
     collected = lax.fori_loop(0, BLOCKS, one_block, jnp.zeros((8, LANES), F32))
-    for member in range(sums.shape[0]):
-        sums[member] = collected
+    sums[...] = collected
 
 
 def middle_kernel(
-    records,
-    tails,
-    position,
+    facts,
     sums,
     feature,
     response,
@@ -255,15 +255,11 @@
     rim,
     window,
 ):
-    first = position[0] * BLOCKS
     total = jnp.sum(sums[...], axis=0)
     line = lax.broadcasted_iota(jnp.int32, (8, LANES), 0)
     lane = lax.broadcasted_iota(jnp.int32, (8, LANES), 1)
-    used = jnp.full((8, LANES), KM, jnp.int32)
-    for b in range(BLOCKS):
-        _, _, own = block_facts(records, tails, first + b)
-        used = jnp.where(line == b, own, used)
-    scale = (lane < used).astype(F32) * lax.rsqrt(total / C + EPSILON)
+    used = facts[2 * BLOCKS :, :]
+    scale = jnp.where(lane.astype(F32) < used, 1.0, 0.0) * lax.rsqrt(total / C + EPSILON)
     inner = pltpu.roll(total, BLOCKS, 0) * scale / C
     both = jnp.where(line < BLOCKS, scale, pltpu.roll(inner, BLOCKS, 0))
     columns = jnp.concatenate([both] * 16, axis=0).T
@@ -285,7 +281,7 @@
         reply[here, :] = (d_gated * query_feature).astype(BF16)
     gain_sum[...] = gain_total
 
-    _, carry_next, _ = block_facts(records, tails, first)
+    carry_next = carry_next_of(facts, 0)
     window[:KM, :] = reply[:KM, :].astype(F32)
     window[KM:, :] = reply[KM : KM + UNIT, :].astype(F32) * carry_next
     totals = [jnp.zeros((8, LANES), F32) for _ in range(4)]
@@ -300,10 +296,8 @@
 
 
 def backward_kernel(
-    slot,
-    records,
-    tails,
-    position,
+    source,
+    facts,
     query,
     reply,
     rim_back,
@@ -324,7 +318,6 @@
     tap_total,
     spread,
 ):
-    first = position[0] * BLOCKS
     mixed[:KM, :] = rim[:KM, :].astype(F32)
     replies[ROWS:, :] = rim_back[:KM, :].astype(F32)
     for b in range(BLOCKS):
@@ -338,7 +331,7 @@
     lag_total[...] = jnp.zeros_like(lag_total)
 
     def one_block(b, unused):
-        carry, carry_next, _ = block_facts(records, tails, first + b)
+        carry, carry_next = carry_of(facts, b), carry_next_of(facts, b)
         here = pl.ds(pl.multiple_of(b * KM, KM), KM)
         after = pl.ds(pl.multiple_of((b + 1) * KM, KM), KM)
         pair[:KM, :] = replies[here, :]
@@ -369,7 +362,7 @@
 
     tap_total[...] = jnp.zeros_like(tap_total)
     for b in range(BLOCKS):
-        carry, carry_next, _ = block_facts(records, tails, first + b)
+        carry, carry_next = carry_of(facts, b), carry_next_of(facts, b)
         here = slice(b * KM, (b + 1) * KM)
         for s in range(3):
             if b == 0:
@@ -400,17 +393,17 @@
         pieces = jnp.concatenate([part[rows] for part in mixer_parts] + [turned[rows]], axis=0)
         back[shard, 3 * CAP * UNIT :, :] = pieces.astype(BF16)
 
-    def move(unit, carry):
-        to = slot[unit]
-        shard = to // CAP
-        rank = to % CAP
+    def move(place, carry):
+        unit = source[place]
+        shard = place // CAP
+        rank = place % CAP
         for s in range(3):
             back[shard, pl.ds(pl.multiple_of((s * CAP + rank) * UNIT, UNIT), UNIT), :] = spread[
                 s, pl.ds(pl.multiple_of(unit * UNIT, UNIT), UNIT), :
             ]
         return carry
 
-    lax.fori_loop(0, UNITS_DEV, move, 0)
+    lax.fori_loop(0, SHARDS * CAP, move, 0)
 
 
 def finish_kernel(slot, returned, stream_grad, grads):
@@ -432,6 +425,145 @@
     pieces = total[24:32]
     grads[:, KM:] = pieces + pltpu.roll(pieces, LANES - 32, 1) + pltpu.roll(pieces, LANES - 64, 1)
 
+MESH = pl.DeviceIdType.MESH
+
+
+def remote_call(kernel, out_shape, scratch, collective, *operands, scalars=0):
+    return pl.pallas_call(
+        kernel,
+        out_shape=out_shape,
+        in_specs=[SMEM] * scalars + [VMEM] * (len(operands) - scalars),
+        out_specs=jax.tree.map(lambda _: VMEM, out_shape),
+        scratch_shapes=scratch,
+        compiler_params=pltpu.CompilerParams(collective_id=collective, has_side_effects=True),
+    )(*operands)
+
+
+def shard_peers():
+    member = lax.axis_index("fsdp")
+    me = lax.axis_index("seq")
+    row, half = me // 2, me % 2
+    peers = []
+    for away in (1, 7, 2, 6, 3, 5, 4):
+        peers.append((row + away) % 8 * 2 + half)
+        peers.append((row + away) % 8 * 2 + 1 - half)
+    peers.append(row * 2 + 1 - half)
+    return member, me, peers
+
+
+def greet(devices):
+    barrier = pltpu.get_barrier_semaphore()
+    for device in devices:
+        pl.semaphore_signal(barrier, inc=1, device_id=device, device_id_type=MESH)
+
+
+def met(count):
+    pl.semaphore_wait(pltpu.get_barrier_semaphore(), count)
+
+
+def finish_copies(copies):
+    for copy in copies:
+        copy.wait_send()
+    for copy in copies:
+        copy.wait_recv()
+
+
+def deal(blocks, out, sent, came, own):
+    member, me, peers = shard_peers()
+    mine = pltpu.make_async_copy(blocks.at[me], out.at[me], own)
+    mine.start()
+    copies = []
+    for number, to in enumerate(peers):
+        copy = pltpu.make_async_remote_copy(
+            src_ref=blocks.at[to],
+            dst_ref=out.at[me],
+            send_sem=sent.at[number],
+            recv_sem=came.at[number],
+            device_id=(member, to),
+            device_id_type=MESH,
+        )
+        copy.start()
+        copies.append(copy)
+    mine.wait()
+    finish_copies(copies)
+
+
+def pass_on(source, target, sent, came, by):
+    member = lax.axis_index("fsdp")
+    to = lax.rem(lax.axis_index("seq") + SHARDS + by, SHARDS)
+    copy = pltpu.make_async_remote_copy(
+        src_ref=source,
+        dst_ref=target,
+        send_sem=sent,
+        recv_sem=came,
+        device_id=(member, to),
+        device_id_type=MESH,
+    )
+    copy.start()
+    copy.wait()
+
+
+def exchange_kernel(blocks, out, sent, came, own):
+    member, _, peers = shard_peers()
+    greet([(member, to) for to in peers])
+    met(len(peers))
+    deal(blocks, out, sent, came, own)
+
+
+def middle_remote_kernel(
+    facts, packed, rim, mixer, small, out_grad,
+    feature, out, query, reply, gain_sum, rim_back,
+    response, collected, sums, rim_out, window3, mixed, pair, shifted, window,
+    sent, came, own, rim_sent, rim_came,
+):
+    members = sums.shape[0]
+    member = lax.axis_index("fsdp")
+    me = lax.axis_index("seq")
+    others = [(lax.rem(member + away, members), me) for away in range(1, members)]
+    greet(others + [(member, lax.rem(me + 1, SHARDS))])
+    forward_kernel(
+        facts, packed, rim, mixer, small, out_grad,
+        feature, response, collected, window3, mixed, pair, shifted,
+    )
+    met(members)
+    mine = pltpu.make_async_copy(collected, sums.at[member], own)
+    mine.start()
+    copies = []
+    for number, device in enumerate(others):
+        copy = pltpu.make_async_remote_copy(
+            src_ref=collected,
+            dst_ref=sums.at[member],
+            send_sem=sent.at[number],
+            recv_sem=came.at[number],
+            device_id=device,
+            device_id_type=MESH,
+        )
+        copy.start()
+        copies.append(copy)
+    mine.wait()
+    finish_copies(copies)
+    middle_kernel(
+        facts, sums, feature, response, mixer, small, out_grad,
+        out, query, reply, gain_sum, rim_out, window,
+    )
+    pass_on(rim_out, rim_back, rim_sent, rim_came, -1)
+
+
+def exchange(blocks, collective):
+    if INTERPRET:
+        return lax.all_to_all(blocks, "seq", split_axis=0, concat_axis=0, tiled=True)
+    return remote_call(
+        exchange_kernel,
+        shape(*blocks.shape, dtype=blocks.dtype),
+        [
+            pltpu.SemaphoreType.DMA((SHARDS,)),
+            pltpu.SemaphoreType.DMA((SHARDS,)),
+            pltpu.SemaphoreType.DMA,
+        ],
+        collective,
+        blocks,
+    )
+
 
 def routing(unit_dest, position):
     target = (unit_dest // UNITS_DEV).reshape(SHARDS, UNITS_DEV)
@@ -442,7 +574,9 @@
     arrive = (jnp.arange(SHARDS, dtype=jnp.int32)[:, None] * CAP + rank).reshape(-1)
     match = unit_dest[None, :] == (position * UNITS_DEV + ids)[:, None]
     packed_slot = jnp.sum(jnp.where(match, arrive[None, :], 0), axis=1)
-    return own_slot.astype(jnp.int32), packed_slot.astype(jnp.int32)
+    places = jnp.arange(SHARDS * CAP, dtype=jnp.int32)[:, None]
+    back_source = jnp.sum(jnp.where(packed_slot[None, :] == places, ids[None, :], 0), axis=1)
+    return own_slot, packed_slot, back_source
 
 
 def body(
@@ -450,7 +584,7 @@
 ):
     members = lax.axis_size("fsdp")
     position = lax.axis_index("seq").astype(jnp.int32)
-    own_slot, packed_slot = routing(unit_dest, position)
+    own_slot, packed_slot, back_source = routing(unit_dest, position)
     where = position.reshape(1)
     filters = jnp.concatenate(
         [
@@ -461,17 +595,19 @@
         ],
         axis=0,
     ).T
-    outgoing = call(
+    outgoing, facts = call(
         pack_kernel,
-        shape(SHARDS, OUT_UNITS * UNIT, LANES),
+        (shape(SHARDS, OUT_UNITS * UNIT, LANES), shape(16, LANES, dtype=F32)),
         [],
         own_slot,
+        record_blocks,
+        tail_rows,
+        where,
         streams,
         filters,
-        scalars=1,
-    )
-    arrived = lax.all_to_all(outgoing, "seq", split_axis=0, concat_axis=0, tiled=True)
-    facts = (record_blocks, tail_rows, where)
+        scalars=4,
+    )
+    arrived = exchange(outgoing, 0)
     packed, mixer, small, rim_out = call(
         unpack_kernel,
         (
@@ -482,53 +618,45 @@
         ),
         [pltpu.VMEM((2, LANES, LANES), F32)],
         packed_slot,
-        *facts,
+        facts,
         arrived,
-        scalars=4,
+        scalars=1,
     )
     rim = lax.ppermute(rim_out, "seq", [(i, i + 1) for i in range(SHARDS - 1)])
-    feature, response, sums = call(
-        forward_kernel,
+    feature, out, query, reply, gain_sum, rim_back = remote_call(
+        middle_remote_kernel,
         (
             shape(3, ROWS, LANES),
-            shape(ROWS, LANES, dtype=F32),
-            shape(members, 8, LANES, dtype=F32),
-        ),
-        [
-            pltpu.VMEM((3, UNIT + KM, LANES), F32),
-            pltpu.VMEM((ROWS + KM, LANES), F32),
-            pltpu.VMEM((2 * KM, LANES), F32),
-            pltpu.VMEM((8, 2 * KM, LANES), F32),
-        ],
-        *facts,
-        packed,
-        rim,
-        mixer,
-        small,
-        out_grad,
-        scalars=3,
-    )
-    sums = lax.all_to_all(sums, "fsdp", split_axis=0, concat_axis=0, tiled=True)
-    out, query, reply, gain_sum, rim_back_out = call(
-        middle_kernel,
-        (
             shape(ROWS, LANES),
             shape(ROWS, LANES),
             shape(ROWS, LANES),
             shape(8, LANES, dtype=F32),
             shape(RIM, LANES),
         ),
-        [pltpu.VMEM((KM + UNIT, LANES), F32)],
-        *facts,
-        sums,
-        feature,
-        response,
+        [
+            pltpu.VMEM((ROWS, LANES), F32),
+            pltpu.VMEM((8, LANES), F32),
+            pltpu.VMEM((members, 8, LANES), F32),
+            pltpu.VMEM((RIM, LANES), BF16),
+            pltpu.VMEM((3, UNIT + KM, LANES), F32),
+            pltpu.VMEM((ROWS + KM, LANES), F32),
+            pltpu.VMEM((2 * KM, LANES), F32),
+            pltpu.VMEM((8, 2 * KM, LANES), F32),
+            pltpu.VMEM((KM + UNIT, LANES), F32),
+            pltpu.SemaphoreType.DMA((members,)),
+            pltpu.SemaphoreType.DMA((members,)),
+            pltpu.SemaphoreType.DMA,
+            pltpu.SemaphoreType.DMA,
+            pltpu.SemaphoreType.DMA,
+        ],
+        1,
+        facts,
+        packed,
+        rim,
         mixer,
         small,
         out_grad,
-        scalars=3,
-    )
-    rim_back = lax.ppermute(rim_back_out, "seq", [(i + 1, i) for i in range(SHARDS - 1)])
+    )
     returning = call(
         backward_kernel,
         shape(SHARDS, BACK_UNITS * UNIT, LANES),
@@ -543,8 +671,8 @@
             pltpu.VMEM((32, 8, LANES), F32),
             pltpu.VMEM((3, ROWS, LANES), BF16),
         ],
-        packed_slot,
-        *facts,
+        back_source,
+        facts,
         query,
         reply,
         rim_back,
@@ -554,9 +682,9 @@
         mixer,
         small,
         gain_sum,
-        scalars=4,
-    )
-    returned = lax.all_to_all(returning, "seq", split_axis=0, concat_axis=0, tiled=True)
+        scalars=1,
+    )
+    returned = exchange(returning, 2)
     stream_grad, grads = call(
         finish_kernel,
         (shape(3, ROWS, LANES), shape(8, 2 * LANES, dtype=F32)),

time: 155 us -> 133 us (0.86)
  Pallas kernels: 25 us -> 112 us
  blocking collectives: 58.1 us -> 0 us
  waiting for transfers between devices: 42.5 us -> 1.4 us
  starting transfers between devices: 19.5 us -> 8.41 us
    pallas_call x0 -> x3, Pallas kernels: none -> 94.5 us  [remote_call(): pl.pallas_call(kernel, out_shape=out_shape, in_specs=[SMEM] * scalars + [...]
    all_to_all x2 -> x0, blocking collectives: 58.1 us -> none  [the longest x1 43.3 us: body(): lax.all_to_all(returning, 'seq', split_axis=0, concat_axis=0, tiled=True)]
    all_to_all x1 -> x0, waiting for transfers between devices: 30.6 us -> none  [body(): lax.all_to_all(outgoing, 'seq', split_axis=0, concat_axis=0, tiled=True)]
    all_to_all x1 -> x0, starting transfers between devices: 15.6 us -> none  [body(): lax.all_to_all(outgoing, 'seq', split_axis=0, concat_axis=0, tiled=True)]
    ppermute x1 -> x0, waiting for transfers between devices: 9.97 us -> none  [body(): lax.ppermute(rim_back_out, 'seq', [(i + 1, i) for i in range(SHARDS - 1)])]
    pallas_call x6 -> x4, Pallas kernels: 25 us -> 17 us  [call(): pl.pallas_call(kernel, out_shape=out_shape, in_specs=[SMEM] * scalars + [...]
    ppermute x1, starting transfers between devices: 2.53 us -> 8.41 us  [body(): rim = lax.ppermute(rim_out, 'seq', [(i, i + 1) for i in range(SHARDS - 1)])]
    unnamed x18 -> x19, local copies, waits for them, and re-layouts: 3.42 us -> 4.28 us
  transfers between devices with their start and end apart: 3 -> 1, of which waited for: 3 -> 1; matrix products, arithmetic and copies ran while one was open for 1% -> 0% of each run, Pallas kernels for 0% -> 0%
where the time goes in v3:
time: 133 us; the launch traced here: 132 us
  Pallas kernels  112 us (84%)
  starting transfers between devices  8.41 us (6%)
  local copies, waits for them, and re-layouts  6.83 us (5%)
  other arithmetic  3.05 us (2%)
  waiting for transfers between devices  1.4 us (1%)
    pallas_call x3, Pallas kernels, remote_call(): pl.pallas_call(kernel, out_shape=out_shape, in_specs=[SMEM] * scalars + [...  94.5 us
    pallas_call x4, Pallas kernels, call(): pl.pallas_call(kernel, out_shape=out_shape, in_specs=[SMEM] * scalars + [...  17 us
    ppermute x1, starting transfers between devices, body(): rim = lax.ppermute(rim_out, 'seq', [(i, i + 1) for i in range(SHARDS - 1)])  8.41 us
    unnamed x19, local copies, waits for them, and re-layouts  4.28 us
  transfers between devices with their start and end apart: 1, of which 1 were waited for; matrix products, arithmetic and copies ran while one was open for 0% of the time, Pallas kernels for 0%

profile of v3, /device:TPU:2, one launch (start us, length us, event | category | flops | bytes accessed | tf_op | source)
XLA Modules:
  0.0 132.0 jit_solution(1370028723092251940)
XLA Ops:
  0.7 0.0 copy-start.4
  0.7 0.7 copy-done.4
  1.4 0.6 copy-done.7
  2.0 0.1 copy.23
  2.1 0.1 reshape.62
  2.2 0.5 convert_reduce_fusion
  2.6 0.5 fusion.2.slot
  3.2 0.1 broadcast_add_fusion
  3.2 0.1 add.39
  3.3 0.6 copy-done.3
  3.9 0.1 copy.22
  4.0 0.1 pad.3.clone
  4.0 0.5 copy-done.5
  4.6 0.7 maximum_bitcast_fusion.filters
  5.2 2.6 %shard_map.119 = (bf16[16,208,128]{2,1,0:T(8,128)(2,1)}, f32[16,128]{1,0:T(8,128)}) custom-call(s32[32]{0:T(128)} %fusion.2.slot, s32[3]{0:T(128)} %records.1, s32[3]{0:T(128)} %tails.1, s32[1]{0:T(128)} %bitcast.1.position, bf16[3,512,128]{2,1,0:T(8,128)(2,1)} %streams.1, f32[8,256]{1,0:T(8,128)} %maximum_bitcast_fusion.filters), custom_call_target="tpu_custom_call" | custom-call | tf_op jit(solution)/shard_map/pallas_call | solution.py:34
  7.8 36.4 %shard_map.120.arrived = bf16[16,208,128]{2,1,0:T(8,128)(2,1)} custom-call(bf16[16,208,128]{2,1,0:T(8,128)(2,1)} %get-tuple-element.20.blocks), custom_call_target="tpu_custom_call" | custom-call | tf_op jit(solution)/shard_map/pallas_call | solution.py:432
  44.2 0.7 select_reduce_fusion.slot
  44.9 2.5 %shard_map.121 = (bf16[3,512,128]{2,1,0:T(8,128)(2,1)}, f32[128,128]{1,0:T(8,128)}, f32[32,128]{1,0:T(8,128)}, bf16[176,128]{1,0:T(8,128)(2,1)}) custom-call(s32[32]{0:T(128)} %select_reduce_fusion.slot, f32[16,128]{1,0:T(8,128)} %get-tuple-element.19.facts, bf16[16,208,128]{2,1,0:T(8,128)(2,1)} %shard_map.120.arrived), custom_call_target="tpu_custom_call" | custom-call | tf_op jit(solution)/shard_map/pallas_call | solution.py:34
  47.4 8.4 %collective-permute-start = (bf16[176,128]{1,0:T(8,128)(2,1)}, bf16[176,128]{1,0:T(8,128)(2,1)S(1)}, u32[]{:S(2)}, u32[]{:S(2)}) collective-permute-start(bf16[176,128]{1,0:T(8,128)(2,1)} %get-tuple-element.22), channel_id=1, source_target_pairs={{0,1},{1,2},{2,3},{3,4},{4,5},{5,6},{6,7},{7,8},{8,9},{9,10},{10,1... | collective-permute-start | bytes 135176 | tf_op jit(solution)/shard_map/ppermute | solution.py:625
  55.9 0.0 copy-done.6
  55.9 0.6 select_reduce_fusion.1.source
  56.5 1.4 %collective-permute-done.rim = bf16[176,128]{1,0:T(8,128)(2,1)S(1)} collective-permute-done((bf16[176,128]{1,0:T(8,128)(2,1)}, bf16[176,128]{1,0:T(8,128)(2,1)S(1)}, u32[]{:S(2)}, u32[]{:S(2)}) %collective-permute-start) | collective-permute-done | bytes 45088 | tf_op jit(solution)/shard_map/ppermute | solution.py:625
  57.9 0.6 copy-done
  58.5 21.8 %shard_map.122 = (bf16[3,512,128]{2,1,0:T(8,128)(2,1)}, bf16[512,128]{1,0:T(8,128)(2,1)}, bf16[512,128]{1,0:T(8,128)(2,1)}, bf16[512,128]{1,0:T(8,128)(2,1)}, f3...) custom-call(f32[16,128]{1,0:T(8,128)} %get-tuple-element.19.facts, bf16[3,512,128]{2,1,0:T(8,128)(2,1)} %get-tuple-element.21.packed, ...), custom_call_target="tpu_custom_call" | custom-call | tf_op jit(solution)/shard_map/pallas_call | solution.py:432
  80.3 9.4 %shard_map.123.blocks = bf16[16,224,128]{2,1,0:T(8,128)(2,1)} custom-call(s32[64]{0:T(128)} %select_reduce_fusion.1.source, f32[16,128]{1,0:T(8,128)} %get-tuple-element.19.facts, bf16[512,128]{1,0:T(8,128)(2,1)} %get-tuple-element.26.query, bf16[512,128]{1,0:T(8,128)(2,1)} %get-tuple-element.27.reply, bf16[176,128]{1,0:T(8,128)(2,1)} %get-tuple-element.28.rim_back, ...), custom_call_target="tpu_custom_call" | custom-call | tf_op jit(solution)/shard_map/pallas_call | solution.py:34
  89.7 36.4 %shard_map.124.returned = bf16[16,224,128]{2,1,0:T(8,128)(2,1)} custom-call(bf16[16,224,128]{2,1,0:T(8,128)(2,1)} %shard_map.123.blocks), custom_call_target="tpu_custom_call" | custom-call | tf_op jit(solution)/shard_map/pallas_call | solution.py:432
  126.1 2.5 %shard_map.125 = (bf16[3,512,128]{2,1,0:T(8,128)(2,1)}, f32[8,256]{1,0:T(8,128)}) custom-call(s32[32]{0:T(128)} %fusion.2.slot, bf16[16,224,128]{2,1,0:T(8,128)(2,1)} %shard_map.124.returned), custom_call_target="tpu_custom_call" | custom-call | tf_op jit(solution)/shard_map/pallas_call | solution.py:34
  128.6 1.5 %slice_reduce_fusion = f32[8]{0:T(128)} fusion(f32[256,8]{0,1:T(8,128)} %bitcast.7), kind=kLoop, calls=%fused_computation.6 | loop fusion | bytes 64 | tf_op jit(solution)/shard_map/slice | solution.py:699
  130.1 0.6 slice.12
  130.7 0.1 copy.24
  130.8 0.6 copy.25
  131.4 0.7 copy.27
  (18 shorter events, 0.1 us)
Async XLA Ops:
  0.7 0.7 copy-start.4
  1.4 0.7 copy-start.7
  3.2 0.7 copy-start.3
  3.9 0.7 copy-start.5
  47.4 8.4 %copy-start.6 = (s32[32]{0:T(128)S(1)}, s32[32]{0:T(128)}, u32[]{:S(2)}) copy-start(s32[32]{0:T(128)} %select_reduce_fusion.slot) | copy-start | bytes 388
  47.4 10.4 %collective-permute-start = (bf16[176,128]{1,0:T(8,128)(2,1)}, bf16[176,128]{1,0:T(8,128)(2,1)S(1)}, u32[]{:S(2)}, u32[]{:S(2)}) collective-permute-start(bf16[176,128]{1,0:T(8,128)(2,1)} %get-tuple-element.22), channel_id=1, source_target_pairs={{0,1},{1,2},{2,3},{3,4},{4,5},{5,6},{6,7},{7,8},{8,9},{9,10},{10,1... | collective-permute-start | bytes 135176 | tf_op jit(solution)/shard_map/ppermute | solution.py:625
  57.9 0.6 copy-start
  126.1 5.3 %copy-start.1 = (bf16[512,128]{1,0:T(8,128)(2,1)S(1)}, bf16[512,128]{1,0:T(8,128)(2,1)}, u32[]{:S(2)}) copy-start(bf16[512,128]{1,0:T(8,128)(2,1)} %get-tuple-element.53) | copy-start | bytes 393220
  128.6 1.5 %copy-start.2 = (f32[8,256]{1,0:T(8,128)S(1)}, f32[8,256]{1,0:T(8,128)}, u32[]{:S(2)}) copy-start(f32[8,256]{1,0:T(8,128)} %get-tuple-element.32) | copy-start | bytes 24580

commit v4 on v3

--- a/solution.py
+++ b/solution.py
@@ -28,6 +28,11 @@
 OUT_UNITS = 3 * CAP + 1
 BACK_UNITS = 3 * CAP + 2
 RIM = KM + 3 * UNIT
+FROM_PACKED = 16
+FROM_OWN = FROM_PACKED + UNITS_DEV
+FROM_BACK = FROM_OWN + UNITS_DEV
+FACTS = FROM_BACK + SHARDS * CAP
+SLOT_ROWS = SHARDS * CAP * UNIT
 
 
 def call(kernel, out_shape, scratch, *operands, scalars=0):
@@ -78,7 +83,7 @@
         rows = jnp.where(line == b, carry, rows)
         rows = jnp.where(line == b + BLOCKS, carry_next, rows)
         rows = jnp.where(line == b + 2 * BLOCKS, used.astype(F32), rows)
-    facts[...] = rows
+    facts[:16, :] = rows
 
 
 def carry_of(facts, b):
@@ -94,12 +99,52 @@
     return jnp.where(rows < facts[pl.ds(b + 2 * BLOCKS, 1), :], 1.0, 0.0)
 
 
+def one_hot(matrix, facts, base):
+    lanes = lax.broadcasted_iota(jnp.int32, (UNIT, LANES), 1)
+    rows = lax.broadcasted_iota(jnp.int32, (UNIT, LANES), 0)
+    offset = (lanes - rows).astype(F32)
+
+    def unit_rows(unit, carry):
+        start = facts[pl.ds(base + unit, 1), :]
+        at = pl.ds(pl.multiple_of(unit * UNIT, UNIT), UNIT)
+        for column in range(0, matrix.shape[1], LANES):
+            picked = jnp.where(offset + column == start, 1.0, 0.0)
+            matrix[at, column : column + LANES] = picked.astype(BF16)
+        return carry
+
+    lax.fori_loop(0, matrix.shape[0] // UNIT, unit_rows, 0)
+
+
+def pick(matrix, table):
+    return jnp.dot(matrix, table, preferred_element_type=F32).astype(BF16)
+
+
+def slots_of(arrived, s):
+    part = arrived[:, s * CAP * UNIT : (s + 1) * CAP * UNIT, :]
+    return part.reshape(SLOT_ROWS, LANES)
+
+
 def fold8(value):
     return jnp.sum(value.reshape(-1, 8, LANES), axis=0)
 
 
-def pack_kernel(slot, records, tails, position, streams, filters, out, facts):
+def pack_kernel(
+    slot, packed_slot, source, records, tails, position, streams, filters, out, facts
+):
     write_facts(facts, records, tails, position[0] * BLOCKS)
+
+    def note(unit, carry):
+        facts[pl.ds(FROM_PACKED + unit, 1), :] = jnp.full((1, LANES), UNIT * packed_slot[unit], F32)
+        facts[pl.ds(FROM_OWN + unit, 1), :] = jnp.full((1, LANES), UNIT * slot[unit], F32)
+        return carry
+
+    def note_source(place, carry):
+        facts[pl.ds(FROM_BACK + place, 1), :] = jnp.full((1, LANES), UNIT * source[place], F32)
+        return carry
+
+    lax.fori_loop(0, UNITS_DEV, note, 0)
+    lax.fori_loop(0, SHARDS * CAP, note_source, 0)
+    out[...] = jnp.zeros(out.shape, BF16)
     taps = filters[...]
     high, middle, low = parts_of(taps[:, KM:])
     lane = lax.broadcasted_iota(jnp.int32, (8, LANES), 1)
@@ -133,18 +178,9 @@
     lax.fori_loop(0, UNITS_DEV, move, 0)
 
 
-def unpack_kernel(slot, facts, arrived, packed, mixer, small, rim, turned):
-    def move(unit, carry):
-        at = slot[unit]
-        shard = at // CAP
-        rank = at % CAP
-        for s in range(3):
-            packed[s, pl.ds(pl.multiple_of(unit * UNIT, UNIT), UNIT), :] = arrived[
-                shard, pl.ds(pl.multiple_of((s * CAP + rank) * UNIT, UNIT), UNIT), :
-            ]
-        return carry
-
-    lax.fori_loop(0, UNITS_DEV, move, 0)
+def unpack_kernel(facts, matrix, arrived, packed, mixer, small, rim, turned):
+    for s in range(3):
+        packed[s] = pick(matrix[...], slots_of(arrived, s))
     for shard in range(SHARDS):
         panel = arrived[shard, 3 * CAP * UNIT :, :].astype(F32)
         turned[0, shard * 8 : shard * 8 + 8, :] = panel[:8]
@@ -258,7 +294,7 @@
     total = jnp.sum(sums[...], axis=0)
     line = lax.broadcasted_iota(jnp.int32, (8, LANES), 0)
     lane = lax.broadcasted_iota(jnp.int32, (8, LANES), 1)
-    used = facts[2 * BLOCKS :, :]
+    used = facts[2 * BLOCKS : 4 * BLOCKS, :]
     scale = jnp.where(lane.astype(F32) < used, 1.0, 0.0) * lax.rsqrt(total / C + EPSILON)
     inner = pltpu.roll(total, BLOCKS, 0) * scale / C
     both = jnp.where(line < BLOCKS, scale, pltpu.roll(inner, BLOCKS, 0))
@@ -296,7 +332,7 @@
 
 
 def backward_kernel(
-    source,
+    matrix,
     facts,
     query,
     reply,
@@ -393,31 +429,16 @@
         pieces = jnp.concatenate([part[rows] for part in mixer_parts] + [turned[rows]], axis=0)
         back[shard, 3 * CAP * UNIT :, :] = pieces.astype(BF16)
 
-    def move(place, carry):
-        unit = source[place]
-        shard = place // CAP
-        rank = place % CAP
-        for s in range(3):
-            back[shard, pl.ds(pl.multiple_of((s * CAP + rank) * UNIT, UNIT), UNIT), :] = spread[
-                s, pl.ds(pl.multiple_of(unit * UNIT, UNIT), UNIT), :
-            ]
-        return carry
-
-    lax.fori_loop(0, SHARDS * CAP, move, 0)
-
-
-def finish_kernel(slot, returned, stream_grad, grads):
-    def move(unit, carry):
-        at = slot[unit]
-        shard = at // CAP
-        rank = at % CAP
-        for s in range(3):
-            stream_grad[s, pl.ds(pl.multiple_of(unit * UNIT, UNIT), UNIT), :] = returned[
-                shard, pl.ds(pl.multiple_of((s * CAP + rank) * UNIT, UNIT), UNIT), :
-            ]
-        return carry
-
-    lax.fori_loop(0, UNITS_DEV, move, 0)
+    for s in range(3):
+        units = pick(matrix[...], spread[s])
+        back[:, s * CAP * UNIT : (s + 1) * CAP * UNIT, :] = units.reshape(
+            SHARDS, CAP * UNIT, LANES
+        )
+
+
+def finish_kernel(matrix, returned, stream_grad, grads):
+    for s in range(3):
+        stream_grad[s] = pick(matrix[...], slots_of(returned, s))
     total = jnp.zeros((2 * UNIT, LANES), F32)
     for shard in range(SHARDS):
         total = total + returned[shard, 3 * CAP * UNIT :, :].astype(F32)
@@ -484,8 +505,7 @@
         )
         copy.start()
         copies.append(copy)
-    mine.wait()
-    finish_copies(copies)
+    return mine, copies
 
 
 def pass_on(source, target, sent, came, by):
@@ -503,11 +523,20 @@
     copy.wait()
 
 
-def exchange_kernel(blocks, out, sent, came, own):
+def arrive_kernel(
+    facts, blocks,
+    packed, mixer, small, rim,
+    arrived, rim_out, turned, matrix, sent, came, own, rim_sent, rim_came,
+):
     member, _, peers = shard_peers()
     greet([(member, to) for to in peers])
     met(len(peers))
-    deal(blocks, out, sent, came, own)
+    mine, copies = deal(blocks, arrived, sent, came, own)
+    one_hot(matrix, facts, FROM_PACKED)
+    mine.wait()
+    finish_copies(copies)
+    unpack_kernel(facts, matrix, arrived, packed, mixer, small, rim_out, turned)
+    pass_on(rim_out, rim, rim_sent, rim_came, 1)
 
 
 def middle_remote_kernel(
@@ -549,20 +578,25 @@
     pass_on(rim_out, rim_back, rim_sent, rim_came, -1)
 
 
-def exchange(blocks, collective):
-    if INTERPRET:
-        return lax.all_to_all(blocks, "seq", split_axis=0, concat_axis=0, tiled=True)
-    return remote_call(
-        exchange_kernel,
-        shape(*blocks.shape, dtype=blocks.dtype),
-        [
-            pltpu.SemaphoreType.DMA((SHARDS,)),
-            pltpu.SemaphoreType.DMA((SHARDS,)),
-            pltpu.SemaphoreType.DMA,
-        ],
-        collective,
-        blocks,
-    )
+def return_kernel(
+    facts, query, reply, rim_back, feature, packed, rim, mixer, small, gain_sum,
+    stream_grad, grads,
+    back, returned, mixed, replies, pair, shifted, lag_total, d_feature, window, tap_total,
+    spread, to_slots, from_slots, sent, came, own,
+):
+    member, _, peers = shard_peers()
+    greet([(member, to) for to in peers])
+    one_hot(to_slots, facts, FROM_BACK)
+    backward_kernel(
+        to_slots, facts, query, reply, rim_back, feature, packed, rim, mixer, small, gain_sum,
+        back, mixed, replies, pair, shifted, lag_total, d_feature, window, tap_total, spread,
+    )
+    met(len(peers))
+    mine, copies = deal(back, returned, sent, came, own)
+    one_hot(from_slots, facts, FROM_OWN)
+    mine.wait()
+    finish_copies(copies)
+    finish_kernel(from_slots, returned, stream_grad, grads)
 
 
 def routing(unit_dest, position):
@@ -597,32 +631,44 @@
     ).T
     outgoing, facts = call(
         pack_kernel,
-        (shape(SHARDS, OUT_UNITS * UNIT, LANES), shape(16, LANES, dtype=F32)),
+        (shape(SHARDS, OUT_UNITS * UNIT, LANES), shape(FACTS, LANES, dtype=F32)),
         [],
         own_slot,
+        packed_slot,
+        back_source,
         record_blocks,
         tail_rows,
         where,
         streams,
         filters,
-        scalars=4,
-    )
-    arrived = exchange(outgoing, 0)
-    packed, mixer, small, rim_out = call(
-        unpack_kernel,
+        scalars=6,
+    )
+    pair_sems = [
+        pltpu.SemaphoreType.DMA((SHARDS,)),
+        pltpu.SemaphoreType.DMA((SHARDS,)),
+        pltpu.SemaphoreType.DMA,
+    ]
+    packed, mixer, small, rim = remote_call(
+        arrive_kernel,
         (
             shape(3, ROWS, LANES),
             shape(KM, LANES, dtype=F32),
             shape(32, LANES, dtype=F32),
             shape(RIM, LANES),
         ),
-        [pltpu.VMEM((2, LANES, LANES), F32)],
-        packed_slot,
+        [
+            pltpu.VMEM(outgoing.shape, BF16),
+            pltpu.VMEM((RIM, LANES), BF16),
+            pltpu.VMEM((2, LANES, LANES), F32),
+            pltpu.VMEM((ROWS, SLOT_ROWS), BF16),
+            *pair_sems,
+            pltpu.SemaphoreType.DMA,
+            pltpu.SemaphoreType.DMA,
+        ],
+        0,
         facts,
-        arrived,
-        scalars=1,
-    )
-    rim = lax.ppermute(rim_out, "seq", [(i, i + 1) for i in range(SHARDS - 1)])
+        outgoing,
+    )
     feature, out, query, reply, gain_sum, rim_back = remote_call(
         middle_remote_kernel,
         (
@@ -657,10 +703,12 @@
         small,
         out_grad,
     )
-    returning = call(
-        backward_kernel,
-        shape(SHARDS, BACK_UNITS * UNIT, LANES),
+    stream_grad, grads = remote_call(
+        return_kernel,
+        (shape(3, ROWS, LANES), shape(8, 2 * LANES, dtype=F32)),
         [
+            pltpu.VMEM((SHARDS, BACK_UNITS * UNIT, LANES), BF16),
+            pltpu.VMEM((SHARDS, BACK_UNITS * UNIT, LANES), BF16),
             pltpu.VMEM((ROWS + KM, LANES), F32),
             pltpu.VMEM((ROWS + KM, LANES), F32),
             pltpu.VMEM((2 * KM, LANES), F32),
@@ -670,8 +718,11 @@
             pltpu.VMEM((KM + UNIT, LANES), F32),
             pltpu.VMEM((32, 8, LANES), F32),
             pltpu.VMEM((3, ROWS, LANES), BF16),
+            pltpu.VMEM((SLOT_ROWS, ROWS), BF16),
+            pltpu.VMEM((ROWS, SLOT_ROWS), BF16),
+            *pair_sems,
         ],
-        back_source,
+        2,
         facts,
         query,
         reply,
@@ -682,16 +733,6 @@
         mixer,
         small,
         gain_sum,
-        scalars=1,
-    )
-    returned = exchange(returning, 2)
-    stream_grad, grads = call(
-        finish_kernel,
-        (shape(3, ROWS, LANES), shape(8, 2 * LANES, dtype=F32)),
-        [],
-        own_slot,
-        returned,
-        scalars=1,
     )
     turned = grads.T
     mixer_grad = turned[:KM]

time: 133 us -> 122 us (0.917)
  the two profiles are of different devices: /device:TPU:2 before, /device:TPU:1 now
where the time goes in v4:
time: 122 us; the launch traced here: 121 us
  Pallas kernels  110 us (90%)
  local copies, waits for them, and re-layouts  7.28 us (6%)
  other arithmetic  3.23 us (3%)
    pallas_call x3, Pallas kernels, remote_call(): pl.pallas_call(kernel, out_shape=out_shape, in_specs=[SMEM] * scalars + [...  107 us
    unnamed x18, local copies, waits for them, and re-layouts  4.75 us
    pallas_call x1, Pallas kernels, call(): pl.pallas_call(kernel, out_shape=out_shape, in_specs=[SMEM] * scalars + [...  3.27 us

profile of v4, /device:TPU:1, one launch (start us, length us, event | category | flops | bytes accessed | tf_op | source)
XLA Modules:
  0.0 121.4 jit_solution(10597753380468617241)
XLA Ops:
  0.6 0.7 add_select_fusion
  1.3 0.1 reshape.62
  1.4 0.5 convert_reduce_fusion
  1.9 0.5 fusion.2.slot
  2.4 0.0 copy-start.3
  2.4 0.1 broadcast_add_fusion
  2.5 0.1 add.39
  2.6 0.5 copy-done.3
  3.1 0.2 select_reduce_fusion.packed_slot
  3.3 0.6 select_reduce_fusion.1.source
  3.9 0.0 copy-done.5
  3.9 0.7 copy-done.6
  4.6 0.1 copy.23
  4.6 0.0 copy-done.2
  4.7 0.1 copy.22
  4.7 0.1 pad.3.clone
  4.8 0.5 copy-done.4
  5.3 0.7 maximum_bitcast_fusion.filters
  6.0 3.3 %shard_map.119 = (bf16[16,208,128]{2,1,0:T(8,128)(2,1)}, f32[144,128]{1,0:T(8,128)}) custom-call(s32[32]{0:T(128)} %fusion.2.slot, s32[32]{0:T(128)} %copy-done.5, s32[64]{0:T(128)} %select_reduce_fusion.1.source, s32[3]{0:T(128)} %records.1, s32[3]{0:T(128)} %tails.1, s32[1]{0:T(128)} %bitcast.1.position, bf16[3,512,128]{2,1,0:T(8,128)(2,1)} %streams.1, ...), custom_call_target="tpu_custom_call" | custom-call | tf_op jit(solution)/shard_map/pallas_call | solution.py:39
  9.3 44.1 %shard_map.120 = (bf16[3,512,128]{2,1,0:T(8,128)(2,1)}, f32[128,128]{1,0:T(8,128)}, f32[32,128]{1,0:T(8,128)}, bf16[176,128]{1,0:T(8,128)(2,1)}) custom-call(f32[144,128]{1,0:T(8,128)} %get-tuple-element.19.facts, bf16[16,208,128]{2,1,0:T(8,128)(2,1)} %get-tuple-element.20.blocks), custom_call_target="tpu_custom_call" | custom-call | tf_op jit(solution)/shard_map/pallas_call | solution.py:453
  53.4 22.0 %shard_map.121 = (bf16[3,512,128]{2,1,0:T(8,128)(2,1)}, bf16[512,128]{1,0:T(8,128)(2,1)}, bf16[512,128]{1,0:T(8,128)(2,1)}, bf16[512,128]{1,0:T(8,128)(2,1)}, f3...) custom-call(f32[144,128]{1,0:T(8,128)} %get-tuple-element.19.facts, bf16[3,512,128]{2,1,0:T(8,128)(2,1)} %get-tuple-element.21.packed, ...), custom_call_target="tpu_custom_call" | custom-call | tf_op jit(solution)/shard_map/pallas_call | solution.py:453
  75.5 0.0 copy-start
  75.5 40.7 %shard_map.122 = (bf16[3,512,128]{2,1,0:T(8,128)(2,1)}, f32[8,256]{1,0:T(8,128)}) custom-call(f32[144,128]{1,0:T(8,128)} %get-tuple-element.19.facts, bf16[512,128]{1,0:T(8,128)(2,1)} %get-tuple-element.26.query, bf16[512,128]{1,0:T(8,128)(2,1)} %get-tuple-element.27.reply, bf16[176,128]{1,0:T(8,128)(2,1)} %get-tuple-element.28.rim_back, ...), custom_call_target="tpu_custom_call" | custom-call | tf_op jit(solution)/shard_map/pallas_call | solution.py:453
  116.2 0.0 copy-start.1
  116.2 1.3 %slice.12 = f32[128,8]{0,1:T(8,128)} slice(f32[256,8]{0,1:T(8,128)} %bitcast.7), slice={[0:128], [0:8]} | slice | bytes 8192 | tf_op jit(solution)/shard_map/slice | solution.py:738
  117.5 0.0 copy-done.1
  117.5 0.1 copy.24
  117.6 0.6 copy.25
  118.2 0.7 slice_reduce_fusion
  118.9 0.0 copy-done
  118.9 0.7 copy.28
  119.6 1.8 %copy.29 = bf16[3,512,128]{2,1,0:T(8,128)(2,1)} copy(bf16[3,512,128]{2,1,0:T(8,128)(2,1)} %get-tuple-element.54) | data formatting | bytes 786432
  (12 shorter events, 0.1 us)
Async XLA Ops:
  2.4 0.7 copy-start.3
  2.5 2.2 %copy-start.2 = (f32[7,3,8]{2,0,1:T(8,128)S(1)}, f32[7,3,8]{2,0,1:T(8,128)}, u32[]{:S(2)}) copy-start(f32[7,3,8]{2,0,1:T(8,128)} %param.13) | copy-start | bytes 2020
  3.3 0.6 copy-start.5
  3.9 0.7 copy-start.6
  4.7 0.7 copy-start.4
  75.5 43.4 %copy-start = (bf16[512,128]{1,0:T(8,128)(2,1)S(1)}, bf16[512,128]{1,0:T(8,128)(2,1)}, u32[]{:S(2)}) copy-start(bf16[512,128]{1,0:T(8,128)(2,1)} %get-tuple-element.53) | copy-start | bytes 393220
  116.2 1.3 %copy-start.1 = (f32[8,256]{1,0:T(8,128)S(1)}, f32[8,256]{1,0:T(8,128)}, u32[]{:S(2)}) copy-start(f32[8,256]{1,0:T(8,128)} %get-tuple-element.32) | copy-start | bytes 24580

commit v5 on v4

--- a/solution.py
+++ b/solution.py
@@ -332,6 +332,7 @@
 
 
 def backward_kernel(
+    early,
     matrix,
     facts,
     query,
@@ -365,42 +366,12 @@
         d_feature[s, ROWS:, :] = rim_back[KM + s * UNIT : KM + (s + 1) * UNIT, :].astype(F32)
     d_feature[0, :ROWS, :] = query[...].astype(F32)
     lag_total[...] = jnp.zeros_like(lag_total)
-
-    def one_block(b, unused):
-        carry, carry_next = carry_of(facts, b), carry_next_of(facts, b)
-        here = pl.ds(pl.multiple_of(b * KM, KM), KM)
-        after = pl.ds(pl.multiple_of((b + 1) * KM, KM), KM)
-        pair[:KM, :] = replies[here, :]
-        pair[KM:, :] = replies[after, :] * carry_next
-        for s in range(8):
-            shifted[s, : 2 * KM - 8, :] = pair[s : 2 * KM - 8 + s, :]
-        total = jnp.zeros((KM, LANES), F32)
-        for s in range(8):
-            for k in range(16):
-                lag = 8 * k + s
-                total = total + mixer[lag : lag + 1, :] * shifted[s, 8 * k : 8 * k + KM, :]
-        d_feature[1, here, :] = (total * feature[2, here, :].astype(F32)).astype(BF16).astype(F32)
-        d_feature[2, here, :] = (total * feature[1, here, :].astype(F32)).astype(BF16).astype(F32)
-        pair[:KM, :] = mixed[here, :] * carry
-        pair[KM:, :] = mixed[after, :]
-        for s in range(8):
-            shifted[s, 8:, :] = pair[8 - s : 2 * KM - s, :]
-        own = replies[here, :]
-        for s in range(8):
-            for k in range(16):
-                lag = 8 * k + s
-                lag_total[lag] = lag_total[lag] + fold8(
-                    own * shifted[s, KM - 8 * k : 2 * KM - 8 * k, :]
-                )
-        return unused
-
-    lax.fori_loop(0, BLOCKS, one_block, 0)
-
     tap_total[...] = jnp.zeros_like(tap_total)
-    for b in range(BLOCKS):
-        carry, carry_next = carry_of(facts, b), carry_next_of(facts, b)
-        here = slice(b * KM, (b + 1) * KM)
-        for s in range(3):
+
+    def one_field(s):
+        for b in range(BLOCKS):
+            carry, carry_next = carry_of(facts, b), carry_next_of(facts, b)
+            here = slice(b * KM, (b + 1) * KM)
             if b == 0:
                 tail = rim[KM + s * UNIT : KM + (s + 1) * UNIT, :].astype(F32)
             else:
@@ -418,6 +389,51 @@
                 row = tap * 3 + s
                 total = total + small[row : row + 1, :] * window[tap : tap + KM, :]
             spread[s, here, :] = total.astype(BF16)
+        units = pick(matrix[...], spread[s])
+        back[:, s * CAP * UNIT : (s + 1) * CAP * UNIT, :] = units.reshape(
+            SHARDS, CAP * UNIT, LANES
+        )
+
+    def mixed_block(b, unused):
+        carry_next = carry_next_of(facts, b)
+        here = pl.ds(pl.multiple_of(b * KM, KM), KM)
+        after = pl.ds(pl.multiple_of((b + 1) * KM, KM), KM)
+        pair[:KM, :] = replies[here, :]
+        pair[KM:, :] = replies[after, :] * carry_next
+        for s in range(8):
+            shifted[s, : 2 * KM - 8, :] = pair[s : 2 * KM - 8 + s, :]
+        total = jnp.zeros((KM, LANES), F32)
+        for s in range(8):
+            for k in range(16):
+                lag = 8 * k + s
+                total = total + mixer[lag : lag + 1, :] * shifted[s, 8 * k : 8 * k + KM, :]
+        d_feature[1, here, :] = (total * feature[2, here, :].astype(F32)).astype(BF16).astype(F32)
+        d_feature[2, here, :] = (total * feature[1, here, :].astype(F32)).astype(BF16).astype(F32)
+        return unused
+
+    def lag_block(b, unused):
+        carry = carry_of(facts, b)
+        here = pl.ds(pl.multiple_of(b * KM, KM), KM)
+        after = pl.ds(pl.multiple_of((b + 1) * KM, KM), KM)
+        pair[:KM, :] = mixed[here, :] * carry
+        pair[KM:, :] = mixed[after, :]
+        for s in range(8):
+            shifted[s, 8:, :] = pair[8 - s : 2 * KM - s, :]
+        own = replies[here, :]
+        for s in range(8):
+            for k in range(16):
+                lag = 8 * k + s
+                lag_total[lag] = lag_total[lag] + fold8(
+                    own * shifted[s, KM - 8 * k : 2 * KM - 8 * k, :]
+                )
+        return unused
+
+    one_field(0)
+    lax.fori_loop(0, BLOCKS, mixed_block, 0)
+    early()
+    lax.fori_loop(0, BLOCKS, lag_block, 0)
+    one_field(1)
+    one_field(2)
 
     tap_total[21] = gain_sum[...]
     mixer_parts = parts_of(jnp.sum(lag_total[...], axis=1).T)
@@ -428,12 +444,6 @@
         rows = slice(shard * 8, shard * 8 + 8)
         pieces = jnp.concatenate([part[rows] for part in mixer_parts] + [turned[rows]], axis=0)
         back[shard, 3 * CAP * UNIT :, :] = pieces.astype(BF16)
-
-    for s in range(3):
-        units = pick(matrix[...], spread[s])
-        back[:, s * CAP * UNIT : (s + 1) * CAP * UNIT, :] = units.reshape(
-            SHARDS, CAP * UNIT, LANES
-        )
 
 
 def finish_kernel(matrix, returned, stream_grad, grads):
@@ -489,15 +499,15 @@
         copy.wait_recv()
 
 
-def deal(blocks, out, sent, came, own):
+def deal(blocks, out, sent, came, own, rows=slice(None)):
     member, me, peers = shard_peers()
-    mine = pltpu.make_async_copy(blocks.at[me], out.at[me], own)
+    mine = pltpu.make_async_copy(blocks.at[me, rows], out.at[me, rows], own)
     mine.start()
     copies = []
     for number, to in enumerate(peers):
         copy = pltpu.make_async_remote_copy(
-            src_ref=blocks.at[to],
-            dst_ref=out.at[me],
+            src_ref=blocks.at[to, rows],
+            dst_ref=out.at[me, rows],
             send_sem=sent.at[number],
             recv_sem=came.at[number],
             device_id=(member, to),
@@ -587,15 +597,23 @@
     member, _, peers = shard_peers()
     greet([(member, to) for to in peers])
     one_hot(to_slots, facts, FROM_BACK)
+    first, rest = slice(0, CAP * UNIT), slice(CAP * UNIT, BACK_UNITS * UNIT)
+    pending = []
+
+    def early():
+        met(len(peers))
+        pending.append(deal(back, returned, sent.at[0], came.at[0], own.at[0], first))
+
     backward_kernel(
-        to_slots, facts, query, reply, rim_back, feature, packed, rim, mixer, small, gain_sum,
-        back, mixed, replies, pair, shifted, lag_total, d_feature, window, tap_total, spread,
-    )
-    met(len(peers))
-    mine, copies = deal(back, returned, sent, came, own)
+        early, to_slots, facts, query, reply, rim_back, feature, packed, rim, mixer, small,
+        gain_sum, back, mixed, replies, pair, shifted, lag_total, d_feature, window, tap_total,
+        spread,
+    )
+    pending.append(deal(back, returned, sent.at[1], came.at[1], own.at[1], rest))
     one_hot(from_slots, facts, FROM_OWN)
-    mine.wait()
-    finish_copies(copies)
+    for mine, copies in pending:
+        mine.wait()
+        finish_copies(copies)
     finish_kernel(from_slots, returned, stream_grad, grads)
 
 
@@ -720,7 +738,9 @@
             pltpu.VMEM((3, ROWS, LANES), BF16),
             pltpu.VMEM((SLOT_ROWS, ROWS), BF16),
             pltpu.VMEM((ROWS, SLOT_ROWS), BF16),
-            *pair_sems,
+            pltpu.SemaphoreType.DMA((2, SHARDS)),
+            pltpu.SemaphoreType.DMA((2, SHARDS)),
+            pltpu.SemaphoreType.DMA((2,)),
         ],
         2,
         facts,

time: 122 us -> 118 us (0.967)
  the two profiles are of different devices: /device:TPU:1 before, /device:TPU:2 now
where the time goes in v5:
time: 118 us; the launch traced here: 117 us
  Pallas kernels  106 us (90%)
  local copies, waits for them, and re-layouts  7.28 us (6%)
  other arithmetic  3.23 us (3%)
    pallas_call x3, Pallas kernels, remote_call(): pl.pallas_call(kernel, out_shape=out_shape, in_specs=[SMEM] * scalars + [...  103 us
    unnamed x18, local copies, waits for them, and re-layouts  4.75 us
    pallas_call x1, Pallas kernels, call(): pl.pallas_call(kernel, out_shape=out_shape, in_specs=[SMEM] * scalars + [...  3.27 us

profile of v5, /device:TPU:2, one launch (start us, length us, event | category | flops | bytes accessed | tf_op | source)
XLA Modules:
  0.0 117.3 jit_solution(5763214594865018040)
XLA Ops:
  0.6 0.7 add_select_fusion
  1.3 0.1 reshape.62
  1.4 0.5 convert_reduce_fusion
  1.9 0.5 fusion.2.slot
  2.4 0.0 copy-start.3
  2.4 0.1 broadcast_add_fusion
  2.5 0.1 add.39
  2.6 0.5 copy-done.3
  3.1 0.2 select_reduce_fusion.packed_slot
  3.3 0.6 select_reduce_fusion.1.source
  3.9 0.0 copy-done.5
  3.9 0.7 copy-done.6
  4.6 0.1 copy.23
  4.6 0.0 copy-done.2
  4.7 0.1 copy.22
  4.7 0.1 pad.3.clone
  4.8 0.5 copy-done.4
  5.3 0.7 maximum_bitcast_fusion.filters
  6.0 3.3 %shard_map.119 = (bf16[16,208,128]{2,1,0:T(8,128)(2,1)}, f32[144,128]{1,0:T(8,128)}) custom-call(s32[32]{0:T(128)} %fusion.2.slot, s32[32]{0:T(128)} %copy-done.5, s32[64]{0:T(128)} %select_reduce_fusion.1.source, s32[3]{0:T(128)} %records.1, s32[3]{0:T(128)} %tails.1, s32[1]{0:T(128)} %bitcast.1.position, bf16[3,512,128]{2,1,0:T(8,128)(2,1)} %streams.1, ...), custom_call_target="tpu_custom_call" | custom-call | tf_op jit(solution)/shard_map/pallas_call | solution.py:39
  9.3 47.2 %shard_map.120 = (bf16[3,512,128]{2,1,0:T(8,128)(2,1)}, f32[128,128]{1,0:T(8,128)}, f32[32,128]{1,0:T(8,128)}, bf16[176,128]{1,0:T(8,128)(2,1)}) custom-call(f32[144,128]{1,0:T(8,128)} %get-tuple-element.19.facts, bf16[16,208,128]{2,1,0:T(8,128)(2,1)} %get-tuple-element.20.blocks), custom_call_target="tpu_custom_call" | custom-call | tf_op jit(solution)/shard_map/pallas_call | solution.py:463
  56.5 18.0 %shard_map.121 = (bf16[3,512,128]{2,1,0:T(8,128)(2,1)}, bf16[512,128]{1,0:T(8,128)(2,1)}, bf16[512,128]{1,0:T(8,128)(2,1)}, bf16[512,128]{1,0:T(8,128)(2,1)}, f3...) custom-call(f32[144,128]{1,0:T(8,128)} %get-tuple-element.19.facts, bf16[3,512,128]{2,1,0:T(8,128)(2,1)} %get-tuple-element.21.packed, ...), custom_call_target="tpu_custom_call" | custom-call | tf_op jit(solution)/shard_map/pallas_call | solution.py:463
  74.6 0.0 copy-start
  74.6 37.5 %shard_map.122 = (bf16[3,512,128]{2,1,0:T(8,128)(2,1)}, f32[8,256]{1,0:T(8,128)}) custom-call(f32[144,128]{1,0:T(8,128)} %get-tuple-element.19.facts, bf16[512,128]{1,0:T(8,128)(2,1)} %get-tuple-element.26.query, bf16[512,128]{1,0:T(8,128)(2,1)} %get-tuple-element.27.reply, bf16[176,128]{1,0:T(8,128)(2,1)} %get-tuple-element.28.rim_back, ...), custom_call_target="tpu_custom_call" | custom-call | tf_op jit(solution)/shard_map/pallas_call | solution.py:463
  112.1 0.0 copy-start.1
  112.1 1.3 %slice.12 = f32[128,8]{0,1:T(8,128)} slice(f32[256,8]{0,1:T(8,128)} %bitcast.7), slice={[0:128], [0:8]} | slice | bytes 8192 | tf_op jit(solution)/shard_map/slice | solution.py:758
  113.5 0.0 copy-done.1
  113.5 0.1 copy.24
  113.6 0.6 copy.25
  114.2 0.7 slice_reduce_fusion
  114.9 0.0 copy-done
  114.9 0.7 copy.28
  115.5 1.8 %copy.29 = bf16[3,512,128]{2,1,0:T(8,128)(2,1)} copy(bf16[3,512,128]{2,1,0:T(8,128)(2,1)} %get-tuple-element.54) | data formatting | bytes 786432
  (12 shorter events, 0.1 us)
Async XLA Ops:
  2.4 0.7 copy-start.3
  2.5 2.2 %copy-start.2 = (f32[7,3,8]{2,0,1:T(8,128)S(1)}, f32[7,3,8]{2,0,1:T(8,128)}, u32[]{:S(2)}) copy-start(f32[7,3,8]{2,0,1:T(8,128)} %param.13) | copy-start | bytes 2020
  3.3 0.6 copy-start.5
  3.9 0.7 copy-start.6
  4.7 0.7 copy-start.4
  74.6 40.3 %copy-start = (bf16[512,128]{1,0:T(8,128)(2,1)S(1)}, bf16[512,128]{1,0:T(8,128)(2,1)}, u32[]{:S(2)}) copy-start(bf16[512,128]{1,0:T(8,128)(2,1)} %get-tuple-element.53) | copy-start | bytes 393220
  112.1 1.3 %copy-start.1 = (f32[8,256]{1,0:T(8,128)S(1)}, f32[8,256]{1,0:T(8,128)}, u32[]{:S(2)}) copy-start(f32[8,256]{1,0:T(8,128)} %get-tuple-element.32) | copy-start | bytes 24580
